TPU v7x, 256 devices: a whole 4x4x8 slice. The times are simulated.
256 devices in a mesh: dp: 8 (over x, core), seq: 32 (over y, z).
Axes of the slice: x: 4, y: 4, z: 8, core: 2. Of those that a mesh axis runs over, the one named last changes fastest.
Arguments:
- tokens: bfloat16 [8, 16384, 1024], P('dp', 'seq'), may hold values from -6 to 6
- cotangent: bfloat16 [8, 16384, 1024], P('dp', 'seq'), may hold values from -6 to 6
- gain_mix: float32 [1024], replicated, may hold values from 0.25 to 1.75
- gain_mlp: float32 [1024], replicated, may hold values from 0.25 to 1.75
- fine_factor: bfloat16 [8, 128, 128], replicated, may hold values from -3.2 to 3.2, as said below
- coarse_factor: bfloat16 [8, 128, 128], replicated, may hold values from -3.2 to 3.2, as said below
- w_gate_up: bfloat16 [1024, 2048], P(('dp', 'seq')), may hold values from -0.1875 to 0.1875
- w_down: bfloat16 [1024, 1024], P(('dp', 'seq')), may hold values from -0.1875 to 0.1875
Outputs:
- layer_out: bfloat16 [8, 16384, 1024], P('dp', 'seq')
- grad_input: bfloat16 [8, 16384, 1024], P('dp', 'seq')
- grad_gate_up: float32 [1024, 2048], P(('dp', 'seq'))
- grad_down: float32 [1024, 1024], P(('dp', 'seq'))
- grad_fine: float32 [8, 128, 128], replicated
- grad_coarse: float32 [8, 128, 128], replicated
- grad_gain_mix: float32 [1024], replicated
- grad_gain_mlp: float32 [1024], replicated
Inputs may be any that keep to these rules, and one draw needn't show every extreme that they name: `fine_factor`: each group's factor is lower triangular: entries above the diagonal are zero. `coarse_factor`: each group's factor is lower triangular: entries above the diagonal are zero.
All inputs are finite; a program needn't handle non-finite values.
Results may differ from a plain program's by a relative error of at most 0.012.
Values may be sent and summed in bfloat16 or wider, within the bound.
A program may use at most 128 MiB of HBM per device.

v0:
```python
import math

import jax
import jax.numpy as jnp
from jax import lax
from jax.sharding import PartitionSpec as P

D = 1024
FF = 1024
NB = 128
NC = 128
GW = 128


epsilon = 1e-05


def widen(values):
    return lax.optimization_barrier(values).astype(jnp.float32)


def norm_rows(values):
    scale_inv = lax.rsqrt(jnp.mean(values * values, axis=-1, keepdims=True) + epsilon)
    return (values * scale_inv, scale_inv)


def norm_back(upstream, normed, scale_inv):
    return scale_inv * (upstream - normed * jnp.mean(upstream * normed, axis=-1, keepdims=True))


def silu_parts(gate_pre):
    squash = jax.nn.sigmoid(gate_pre)
    return (gate_pre * squash, squash * (1.0 + gate_pre * (1.0 - squash)))


def into_coarse(block_data):
    return lax.all_to_all(block_data, "seq", split_axis=1, concat_axis=0, tiled=True)


def into_fine(block_data):
    return lax.all_to_all(block_data, "seq", split_axis=0, concat_axis=1, tiled=True)


def on_device(tokens, cotangent, gain_mix, gain_mlp, fine_factor, coarse_factor, w_gate_up, w_down):
    groups = D // GW
    local_rows = tokens.shape[1]
    block_count = local_rows // NB
    seq_devices = lax.axis_size("seq")
    data_devices = lax.axis_size("dp")
    fine_width = NB // seq_devices
    full_gate_up, full_down = (
        lax.all_gather(w_gate_up, ("dp", "seq"), axis=0, tiled=True),
        lax.all_gather(w_down, ("dp", "seq"), axis=0, tiled=True),
    )
    source = tokens[0].astype(jnp.float32)
    normed_mix, inv_mix = norm_rows(source)
    hidden_in = (normed_mix * gain_mix).astype(jnp.bfloat16)
    gated_in = widen(hidden_in)
    blocked = hidden_in.reshape(block_count, NB, groups, GW)
    fine_mixed = jnp.einsum(
        "gpq,aqgc->apgc", fine_factor, blocked, preferred_element_type=jnp.float32
    ).astype(jnp.bfloat16)
    fine_moved = into_coarse(fine_mixed.reshape(block_count, NB, D)).reshape(
        NC, fine_width, groups, GW
    )
    coarse_mixed = jnp.einsum(
        "gpq,qbgc->pbgc", coarse_factor, fine_moved, preferred_element_type=jnp.float32
    ).astype(jnp.bfloat16)
    mixed = widen(into_fine(coarse_mixed.reshape(NC, fine_width, D))).reshape(local_rows, D)
    after_mix = source + mixed * gated_in
    normed_mlp, inv_mlp = norm_rows(after_mix)
    mlp_in = (normed_mlp * gain_mlp).astype(jnp.bfloat16)
    both = jnp.dot(mlp_in, full_gate_up, preferred_element_type=jnp.float32)
    gate_pre = both[:, :FF]
    upward = both[:, FF:]
    silu_gate, silu_slope = silu_parts(gate_pre)
    activation = (silu_gate * upward).astype(jnp.bfloat16)
    projected = lax.dot_general(
        activation, full_down, (((1,), (1,)), ((), ())), preferred_element_type=jnp.float32
    )
    layer = (after_mix + projected).astype(jnp.bfloat16)
    upstream_out = cotangent[0]
    upstream = upstream_out.astype(jnp.float32)
    back_act = widen(
        jnp.dot(upstream_out, full_down, preferred_element_type=jnp.float32).astype(jnp.bfloat16)
    )
    back_both = jnp.concatenate(
        [back_act * upward * silu_slope, back_act * silu_gate], axis=1
    ).astype(jnp.bfloat16)
    gate_up_part = lax.dot_general(
        mlp_in, back_both, (((0,), (0,)), ((), ())), preferred_element_type=jnp.float32
    )
    down_part = lax.dot_general(
        upstream_out, activation, (((0,), (0,)), ((), ())), preferred_element_type=jnp.float32
    )
    weight_grads = lax.psum_scatter(
        jnp.concatenate([gate_up_part, down_part], axis=1),
        ("dp", "seq"),
        scatter_dimension=0,
        tiled=True,
    )
    back_mlp_in = lax.dot_general(
        back_both, full_gate_up, (((1,), (1,)), ((), ())), preferred_element_type=jnp.float32
    )
    gain_mlp_term = jnp.sum(back_mlp_in * normed_mlp, axis=0)
    back_after = upstream + norm_back(back_mlp_in * gain_mlp, normed_mlp, inv_mlp)
    back_mixed = (back_after * gated_in).astype(jnp.bfloat16)
    mixed_moved = into_coarse(back_mixed.reshape(block_count, NB, D)).reshape(
        NC, fine_width, groups, GW
    )
    back_fine_moved = jnp.einsum(
        "gpq,pbgc->qbgc", coarse_factor, mixed_moved, preferred_element_type=jnp.float32
    ).astype(jnp.bfloat16)
    coarse_term = jnp.einsum(
        "pbgc,qbgc->gpq", mixed_moved, fine_moved, preferred_element_type=jnp.float32
    )
    back_fine = into_fine(back_fine_moved.reshape(NC, fine_width, D)).reshape(
        block_count, NB, groups, GW
    )
    back_blocked = jnp.einsum(
        "gpq,apgc->aqgc", fine_factor, back_fine, preferred_element_type=jnp.float32
    ).reshape(local_rows, D)
    fine_term = jnp.einsum("apgc,aqgc->gpq", back_fine, blocked, preferred_element_type=jnp.float32)
    back_hidden = back_after * mixed + back_blocked
    gain_mix_term = jnp.sum(back_hidden * normed_mix, axis=0)
    grad_in = (back_after + norm_back(back_hidden * gain_mix, normed_mix, inv_mix)).astype(
        jnp.bfloat16
    )
    summed = lax.psum((fine_term, coarse_term, gain_mix_term, gain_mlp_term), ("dp", "seq"))
    all_seqs = data_devices * tokens.shape[0]
    scale_tokens = 1.0 / math.sqrt(all_seqs * NC * NB)
    grad_fine = jnp.tril(summed[0]) * (1.0 / math.sqrt(all_seqs * NC * GW))
    grad_coarse = jnp.tril(summed[1]) * (1.0 / math.sqrt(all_seqs * NB * GW))
    grad_gate_up = weight_grads[:, : 2 * FF] * scale_tokens
    grad_down = weight_grads[:, 2 * FF :] * scale_tokens
    return (
        layer.reshape(1, local_rows, D),
        grad_in.reshape(1, local_rows, D),
        grad_gate_up,
        grad_down,
        grad_fine,
        grad_coarse,
        summed[2] * scale_tokens,
        summed[3] * scale_tokens,
    )


def solution(mesh):
    placed = (
        P("dp", "seq", None),
        P("dp", "seq", None),
        P(),
        P(),
        P(),
        P(),
        P(("dp", "seq"), None),
        P(("dp", "seq"), None),
    )
    return jax.shard_map(
        on_device,
        mesh=mesh,
        in_specs=placed,
        out_specs=(
            P("dp", "seq", None),
            P("dp", "seq", None),
            P(("dp", "seq"), None),
            P(("dp", "seq"), None),
            P(),
            P(),
            P(),
            P(),
        ),
        check_vma=False,
    )
```

profile of v0, /device:TPU:1, one launch (start us, length us, event | category | flops | bytes accessed | tf_op | source)
XLA Modules:
  0.0 647.0 jit_solution(11329390648559127980)
XLA Ops:
  8.7 1.5 convert_bitcast_fusion
  12.5 1.0 copy.85
  13.6 2.6 copy.86
  16.2 37.3 %all_to_all.63 = bf16[4,128,1024]{2,0,1:T(4,128)(2,1)S(1)} all-to-all(bf16[4,128,1024]{2,0,1:T(4,128)(2,1)} %copy.86), channel_id=1, replica_groups=mesh['dp'=8,'seq'=32] {'seq'}, dimensions={1} | all-to-all | bytes 2097152 | tf_op jit(solution)/shard_map/all_to_all | solution.py:37
  53.5 1.5 copy.87
  55.1 2.2 reshape.104
  57.3 1.9 fusion.24
  60.2 2.7 copy.90
  62.9 8.4 %all-to-all-start.1 = ((bf16[128,4,1024]{2,1,0:T(4,128)(2,1)}), bf16[128,4,1024]{2,1,0:T(4,128)(2,1)}, u32[]{:S(2)}, u32[]{:S(2)}) async-start(bf16[128,4,1024]{2,1,0:T(4,128)(2,1)} %copy.90), calls=%async_computation.1 | async-start | bytes 2097152 | tf_op jit(solution)/shard_map/all_to_all | solution.py:41
  71.3 1.3 fusion.11
  72.5 24.4 %all-to-all-done.1 = bf16[128,4,1024]{2,1,0:T(4,128)(2,1)} async-done(((bf16[128,4,1024]{2,1,0:T(4,128)(2,1)}), bf16[128,4,1024]{2,1,0:T(4,128)(2,1)}, u32[]{:S(2)}, u32[]{:S(2)}) %all-to-all-start.1) | async-done | bytes 1048608 | tf_op jit(solution)/shard_map/all_to_all | solution.py:41
  96.9 1.9 copy.91
  99.1 1.9 multiply_reduce_fusion.2
  101.0 23.9 %all-gather.7.cloned.1.call-done = bf16[256,4,1024]{2,1,0:T(4,128)(2,1)} async-done(((bf16[1,4,1024]{2,1,0:T(4,128)(2,1)}), bf16[256,4,1024]{2,1,0:T(4,128)(2,1)}) %all-gather.7.cloned.1.call-update) | async-done | bytes 2097168 | tf_op jit(solution)/shard_map/all_gather | solution.py:53
  124.9 4.0 reshape.122
  128.9 4.2 convolution_convert_fusion.1
  133.1 110.5 %all-gather.5.cloned.1.call-done = bf16[256,4,2048]{2,1,0:T(4,128)(2,1)} async-done(((bf16[1,4,2048]{2,1,0:T(4,128)(2,1)}), bf16[256,4,2048]{2,1,0:T(4,128)(2,1)}) %all-gather.5.cloned.1.call-update) | async-done | bytes 4194320 | tf_op jit(solution)/shard_map/all_gather | solution.py:52
  243.6 6.9 %reshape.120 = bf16[1024,2048]{1,0:T(8,128)(2,1)} reshape(bf16[256,4,2048]{2,1,0:T(4,128)(2,1)} %all-gather.5.cloned.1.call-done) | data formatting | bytes 8388608
  250.6 5.3 fusion.47
  255.9 2.4 fusion.9
  259.1 2.7 multiply_reduce_fusion
  261.8 2.1 fusion.7
  264.7 32.0 %all_to_all.64 = bf16[4,128,1024]{2,0,1:T(4,128)(2,1)S(1)} all-to-all(bf16[4,128,1024]{2,0,1:T(4,128)(2,1)S(1)} %copy.93), channel_id=1, replica_groups=mesh['dp'=8,'seq'=32] {'seq'}, dimensions={1} | all-to-all | bytes 2097152 | tf_op jit(solution)/shard_map/all_to_all | solution.py:37
  296.7 1.5 copy.94
  298.2 2.3 reshape.110
  300.5 1.9 fusion.25
  302.3 1.1 copy.96
  303.4 2.7 copy.97
  306.2 8.2 %all-to-all-start.3 = ((bf16[128,4,1024]{2,1,0:T(4,128)(2,1)}), bf16[128,4,1024]{2,1,0:T(4,128)(2,1)}, u32[]{:S(2)}, u32[]{:S(2)}) async-start(bf16[128,4,1024]{2,1,0:T(4,128)(2,1)} %copy.97), calls=%async_computation.3 | async-start | bytes 2097152 | tf_op jit(solution)/shard_map/all_to_all | solution.py:41
  314.5 3.0 convolution_bitcast_fusion
  317.5 2.5 fusion.27
  320.0 4.8 pad_maximum_fusion
  324.9 1.5 convolution_bitcast_fusion.2
  326.4 13.2 %all-to-all-done.3 = bf16[128,4,1024]{2,1,0:T(4,128)(2,1)} async-done(((bf16[128,4,1024]{2,1,0:T(4,128)(2,1)}), bf16[128,4,1024]{2,1,0:T(4,128)(2,1)}, u32[]{:S(2)}, u32[]{:S(2)}) %all-to-all-start.3) | async-done | bytes 1048608 | tf_op jit(solution)/shard_map/all_to_all | solution.py:41
  339.5 2.6 copy.98
  342.1 2.3 reshape.112
  344.4 2.7 convolution_bitcast_fusion.3
  347.1 1.5 copy-done.5
  348.7 4.3 fusion.26
  352.9 1.9 convolution_bitcast_fusion.1
  354.8 2.0 copy.100
  356.9 3.2 fusion.17
  360.1 77.5 %all-reduce.1 = (f32[1024]{0:T(1024)S(1)}, f32[1024]{0:T(1024)S(1)}) all-reduce(f32[1024]{0:T(1024)S(1)} %get-tuple-element.8, f32[1024]{0:T(1024)S(1)} %get-tuple-element.10), channel_id=1, replica_groups=mesh['dp'=8,'seq'=32] {'dp','seq'}, use_global_device_ids=true, to_apply=%region_8.0 | all-reduce | flops 2048 | bytes 16384 | tf_op jit(solution)/shard_map/psum | solution.py:129
  438.2 3.7 fusion.29
  441.9 193.3 %all-reduce.5.cloned.1.call-done = (f32[1024,3072]{1,0:T(8,128)}, f32[8,128,128]{2,1,0:T(8,128)}, f32[8,128,128]{2,1,0:T(8,128)}) async-done(((f32[1024,3072]{1,0:T(8,128)}, f32[8,128,128]{2,1,0:T(8,128)}, f32[8,128,128]{2,1,0:T(8,128)}), (f32[1024,3072]{1,0:T(8,128)}, f32[8,128,128]{2,1,0:T(8,128)}, f32[8,128,128]{2,1,0:T(8,128)})) %all-reduce.5.cloned.1.call-update) | async-done | bytes 13631504
  635.3 1.5 dynamic-slice_multiply_fusion
  636.7 1.4 dynamic-slice_multiply_fusion.1
  638.2 2.3 select_multiply_fusion
  (63 shorter events, 7.5 us)
Async XLA Ops:
  7.2 50.1 %copy-start = (bf16[8,128,128]{2,1,0:T(8,128)(2,1)S(1)}, bf16[8,128,128]{2,1,0:T(8,128)(2,1)}, u32[]{:S(2)}) copy-start(bf16[8,128,128]{2,1,0:T(8,128)(2,1)} %param.13) | copy-start | bytes 786436
  7.2 117.7 %all-gather.7.cloned.1.call-start = ((), (), s32[]{:S(2)}) async-start(), calls=%async_computation.5 | async-start | bytes 2105344 | tf_op jit(solution)/shard_map/all_gather | solution.py:53
  7.9 235.7 %all-gather.5.cloned.1.call-start = ((), (), s32[]{:S(2)}) async-start(), calls=%async_computation.4 | async-start | bytes 4210688 | tf_op jit(solution)/shard_map/all_gather | solution.py:52
  10.1 1.2 copy-start.2
  10.2 1.5 copy-start.18
  10.2 1.5 copy-start.21
  62.9 34.0 %all-to-all-start.1 = ((bf16[128,4,1024]{2,1,0:T(4,128)(2,1)}), bf16[128,4,1024]{2,1,0:T(4,128)(2,1)}, u32[]{:S(2)}, u32[]{:S(2)}) async-start(bf16[128,4,1024]{2,1,0:T(4,128)(2,1)} %copy.90), calls=%async_computation.1 | async-start | bytes 2097152 | tf_op jit(solution)/shard_map/all_to_all | solution.py:41
  96.9 2.2 copy-start.8
  99.1 1.9 copy-start.6
  133.1 117.5 %copy-start.22 = (f32[1024]{0:T(1024)S(1)}, f32[1024]{0:T(1024)}, u32[]{:S(2)}) copy-start(f32[1024]{0:T(1024)} %param.11) | copy-start | bytes 12292
  250.6 5.3 copy-start.20
  255.9 2.4 copy-start.3
  255.9 3.2 copy-start.10
  258.3 3.5 copy-start.13
  258.3 3.5 copy-start.15
  259.1 2.7 copy-start.9
  259.1 2.7 copy-start.17
  306.2 33.4 %all-to-all-start.3 = ((bf16[128,4,1024]{2,1,0:T(4,128)(2,1)}), bf16[128,4,1024]{2,1,0:T(4,128)(2,1)}, u32[]{:S(2)}, u32[]{:S(2)}) async-start(bf16[128,4,1024]{2,1,0:T(4,128)(2,1)} %copy.97), calls=%async_computation.3 | async-start | bytes 2097152 | tf_op jit(solution)/shard_map/all_to_all | solution.py:41
  314.4 320.9 %all-reduce.5.cloned.1.call-start = ((), (), s32[]{:S(2)}) async-start(), calls=%async_computation.6 | async-start | bytes 27262976
  314.4 3.0 copy-start.4
  314.4 3.0 copy-start.14
  314.5 3.0 copy-start.16
  320.0 4.9 copy-start.11
  320.0 4.9 copy-start.12
  347.1 1.6 copy-start.5
  348.7 4.3 copy-start.7
  348.7 4.3 copy-start.19
  438.2 202.2 %copy-start.1 = (bf16[8,128,128]{2,1,0:T(8,128)(2,1)S(1)}, bf16[8,128,128]{2,1,0:T(8,128)(2,1)}, u32[]{:S(2)}) copy-start(bf16[8,128,128]{2,1,0:T(8,128)(2,1)} %param.13) | copy-start | bytes 786436
Sparse Core Ops, SparseCore 0:
  11.7 113.1 all-gather.6
  128.7 114.8 all-gather.4
  347.2 287.9 all-reduce.4
where the time goes:
time: 649 us; the launch traced here: 647 us
  waiting for transfers between devices  367 us (57%)
  blocking collectives  147 us (23%)
  local copies, waits for them, and re-layouts  43.1 us (7%)
  matrix products  32.6 us (5%)
  other arithmetic  27 us (4%)
  starting transfers between devices  16.7 us (3%)
  between operations  14.1 us (2%)
    unnamed x4, waiting for transfers between devices  195 us
    all_gather x1, waiting for transfers between devices, on_device(): lax.all_gather(w_gate_up, ('dp', 'seq'), axis=0, tiled=True)  111 us
    psum x1, blocking collectives, on_device(): lax.psum((fine_term, coarse_term, gain_mix_term, gain_mlp_term), ('dp', '...  77.5 us
    all_to_all x2, blocking collectives, into_coarse(): lax.all_to_all(block_data, 'seq', split_axis=1, concat_axis=0, tiled=True)  69.3 us
    all_to_all x2, waiting for transfers between devices, into_fine(): lax.all_to_all(block_data, 'seq', split_axis=0, concat_axis=1, tiled=True)  37.5 us
    all_gather x1, waiting for transfers between devices, on_device(): lax.all_gather(w_down, ('dp', 'seq'), axis=0, tiled=True)  23.9 us
    all_to_all x2, starting transfers between devices, into_fine(): lax.all_to_all(block_data, 'seq', split_axis=0, concat_axis=1, tiled=True)  16.6 us
    unnamed x49, local copies, waits for them, and re-layouts  14.5 us
  transfers between devices with their start and end apart: 5, of which 5 were waited for; matrix products, arithmetic and copies ran while one was open for 9% of the time, Pallas kernels for 0%

commit v1 on v0

v1 whole, which is shorter than its diff:
```python
import math

import jax
import jax.numpy as jnp
from jax import lax
from jax.experimental import pallas as pl
from jax.experimental.pallas import tpu as pltpu
from jax.sharding import PartitionSpec as P

D = 1024
FF = 1024
NB = 128
NC = 128
GW = 128
G = 8
NX, NY, NZ = 4, 4, 8
BL = 4
QW = 256
BW = 16
ROWS = BL * NB
WC = 3 * FF
EPS = 1e-05
MESH = pl.DeviceIdType.MESH
F32 = jnp.float32
BF16 = jnp.bfloat16


def place():
    dp = lax.axis_index("dp")
    seq = lax.axis_index("seq")
    return dp // 2, dp % 2, seq // NZ, seq % NZ


def send(src, dst, ssem, rsem, dp, seq):
    return pltpu.make_async_remote_copy(
        src_ref=src,
        dst_ref=dst,
        send_sem=ssem,
        recv_sem=rsem,
        device_id=(dp, seq),
        device_id_type=MESH,
    )


def greet(x, c, y, z):
    bar = pltpu.get_barrier_semaphore()

    def one(dp, seq):
        pl.semaphore_signal(bar, inc=1, device_id=(dp, seq), device_id_type=MESH)

    def plane(k, carry):
        one(2 * x + c, ((y + k // NZ) % NY) * NZ + (z + k % NZ) % NZ)
        return carry

    lax.fori_loop(1, NY * NZ, plane, 0)
    for k in range(1, NX):
        one(2 * ((x + k) % NX) + c, y * NZ + z)
    one(2 * x + 1 - c, y * NZ + z)
    return bar, NY * NZ - 1 + NX - 1 + 1


def dot(a, b, ca=1, cb=0):
    return lax.dot_general(a, b, (((ca,), (cb,)), ((), ())), preferred_element_type=F32)


def exchange_in(src, dst, ssem, rsem, x, c, y, z):
    me = y * NZ + z

    def copy(k):
        ty = (y + k // NZ) % NY
        tz = (z + k % NZ) % NZ
        return send(
            src.at[:, pl.ds(pl.multiple_of(BW * tz, BW), BW), pl.ds(pl.multiple_of(QW * ty, QW), QW)],
            dst.at[pl.ds(BL * me, BL)],
            ssem.at[k],
            rsem.at[k],
            2 * x + c,
            ty * NZ + tz,
        )

    return copy


def exchange_out(src, dst, ssem, rsem, x, c, y, z):
    def copy(k):
        ty = (y + k // NZ) % NY
        tz = (z + k % NZ) % NZ
        to = ty * NZ + tz
        return send(
            src.at[pl.ds(BL * to, BL)],
            dst.at[:, pl.ds(pl.multiple_of(BW * z, BW), BW), pl.ds(pl.multiple_of(QW * y, QW), QW)],
            ssem.at[k],
            rsem.at[k],
            2 * x + c,
            to,
        )

    return copy


def start_all(copy, n):
    def body(k, carry):
        copy(k).start()
        return carry

    lax.fori_loop(1, n, body, 0)


def recv_all(copy, n):
    def body(k, carry):
        copy(k).wait_recv()
        return carry

    lax.fori_loop(1, n, body, 0)


def sent_all(copy, n):
    def body(k, carry):
        copy(k).wait_send()
        return carry

    lax.fori_loop(1, n, body, 0)


def to_rows(src, tall):
    def body(i, carry):
        v = src[pl.ds(8 * i, 8)].reshape(8 * BW, QW).astype(F32)
        at = pl.ds(pl.multiple_of(8 * BW * i, 8 * BW), 8 * BW)
        tall[0, at, :] = v[:, :GW]
        tall[1, at, :] = v[:, GW:]
        return carry

    lax.fori_loop(0, NC // 8, body, 0)


def from_rows(tall, dst):
    def body(i, carry):
        at = pl.ds(pl.multiple_of(8 * BW * i, 8 * BW), 8 * BW)
        v = jnp.concatenate([tall[0, at, :], tall[1, at, :]], axis=1).astype(BF16)
        dst[pl.ds(8 * i, 8)] = v.reshape(8, BW, QW)
        return carry

    lax.fori_loop(0, NC // 8, body, 0)


def own_in(src, dst, x, c, y, z):
    me = y * NZ + z
    dst[pl.ds(BL * me, BL)] = src[
        :, pl.ds(pl.multiple_of(BW * z, BW), BW), pl.ds(pl.multiple_of(QW * y, QW), QW)
    ]


def own_out(src, dst, x, c, y, z):
    me = y * NZ + z
    dst[:, pl.ds(pl.multiple_of(BW * z, BW), BW), pl.ds(pl.multiple_of(QW * y, QW), QW)] = src[
        pl.ds(BL * me, BL)
    ]


def forward_kernel(
    tok, gain, fine, coarse, wgu, wdn,
    mixed, hid, moved, fgu, fdn,
    fm, back, tall, tall2, wz, wrow,
    s_in, r_in, s_out, r_out, s_z, r_z, s_y, r_y, s_x, r_x, s_c, r_c,
):
    x, c, y, z = place()
    dp = 2 * x + c
    seq = y * NZ + z
    bar, count = greet(x, c, y, z)

    wz[pl.ds(z, 1), :, : 2 * FF] = wgu[...].reshape(1, 4, 2 * FF)
    wz[pl.ds(z, 1), :, 2 * FF :] = wdn[...].reshape(1, 4, FF)

    def norm(i, carry):
        a = i // 4
        at = pl.ds(pl.multiple_of((i % 4) * 32, 32), 32)
        v = tok[a, at, :].astype(F32)
        inv = lax.rsqrt(jnp.mean(v * v, axis=-1, keepdims=True) + EPS)
        hid[a, at, :] = ((v * inv) * gain[...]).astype(BF16)
        return carry

    lax.fori_loop(0, BL * 4, norm, 0)

    pl.semaphore_wait(bar, count)

    def z_copy(k):
        tz = (z + k) % NZ
        return send(wz.at[z], wz.at[z], s_z.at[k], r_z.at[k], dp, y * NZ + tz)

    start_all(z_copy, NZ)

    for g in range(G):
        cols = slice(g * GW, (g + 1) * GW)
        for a in range(BL):
            fm[a, :, cols] = dot(fine[g], hid[a, :, cols]).astype(BF16)

    c_in = exchange_in(fm, moved, s_in, r_in, x, c, y, z)
    start_all(c_in, NY * NZ)
    own_in(fm, moved, x, c, y, z)

    recv_all(z_copy, NZ)
    for zz in range(NZ):
        wrow[4 * zz : 4 * zz + 4, :] = wz[zz].astype(F32)
    my = pl.ds(pl.multiple_of(dp * 128 + y * 32, 32), 32)
    fgu[my, :] = wrow[:, : 2 * FF].astype(BF16)
    fdn[my, :] = wrow[:, 2 * FF :].astype(BF16)

    def pair(k, at, ss, rs, tdp, tseq):
        return (
            send(fgu.at[at, :], fgu.at[at, :], ss.at[0, k], rs.at[0, k], tdp, tseq),
            send(fdn.at[at, :], fdn.at[at, :], ss.at[1, k], rs.at[1, k], tdp, tseq),
        )

    y_copies = [pair(k, my, s_y, r_y, dp, ((y + k) % NY) * NZ + z) for k in range(1, NY)]
    for two in y_copies:
        for one in two:
            one.start()
    for two in y_copies:
        for one in two:
            one.wait_recv()

    my_x = pl.ds(pl.multiple_of(dp * 128, 128), 128)
    x_copies = [pair(k, my_x, s_x, r_x, 2 * ((x + k) % NX) + c, seq) for k in range(1, NX)]
    for two in x_copies:
        for one in two:
            one.start()

    def core_copy(k):
        at = pl.ds(pl.multiple_of((2 * ((x + NX - k) % NX) + c) * 128, 128), 128)
        return pair(k, at, s_c, r_c, 2 * x + 1 - c, seq)

    for one in core_copy(0):
        one.start()

    recv_all(c_in, NY * NZ)
    to_rows(moved, tall)
    for b in range(BW):
        for h in range(2):
            v = tall[h, pl.ds(b, NC, stride=BW), :].astype(BF16)
            tall2[h, pl.ds(b, NC, stride=BW), :] = dot(coarse[2 * y + h], v)
    from_rows(tall2, back)
    c_out = exchange_out(back, mixed, s_out, r_out, x, c, y, z)
    start_all(c_out, NY * NZ)
    own_out(back, mixed, x, c, y, z)

    for k in range(1, NX):
        for one in x_copies[k - 1]:
            one.wait_recv()
        for one in core_copy(k):
            one.start()
    recv_all(c_out, NY * NZ)
    for k in range(NX):
        for one in core_copy(k):
            one.wait_recv()
            one.wait_send()
    for two in y_copies + x_copies:
        for one in two:
            one.wait_send()
    sent_all(z_copy, NZ)
    sent_all(c_in, NY * NZ)
    sent_all(c_out, NY * NZ)


def backward_kernel(
    bm, moved, fine, coarse, mlp_in, bboth, cot, act, bafter, mixed, hid, tok, gain, glm,
    gin, ogu, odn, ofine, ocoarse, ogain,
    xin, xout, bfine, bhid, tall, tall2, tallm,
    pbuf, crecv, xrecv, acc, ysend, yrecv, zbuf, zrecv,
    v32, v16, vc, vxs, vx, v2, vys, vy, vz, vzr, az, v3, ay, every,
    gc, gx, gy, gz,
    s_in, r_in, s_out, r_out, s_c, r_c, s_x, r_x, s_y, r_y, s_z, r_z,
    ts, tr, gs, gr,
):
    x, c, y, z = place()
    dp = 2 * x + c
    seq = y * NZ + z
    sib = 2 * x + 1 - c
    bar, count = greet(x, c, y, z)
    pl.semaphore_wait(bar, count)

    c_in = exchange_in(bm, xin, s_in, r_in, x, c, y, z)
    start_all(c_in, NY * NZ)
    own_in(bm, xin, x, c, y, z)

    def part(d, put):
        at = pl.ds(pl.multiple_of(d * 128, 128), 128)
        lhs = mlp_in[:, at]
        for n in range(4):
            cols = slice(512 * n, 512 * n + 512)
            put(cols, dot(lhs, bboth[:, cols], 0, 0))
        lhs = cot[:, at]
        for n in range(2):
            cols = slice(512 * n, 512 * n + 512)
            put(slice(2 * FF + 512 * n, 2 * FF + 512 * n + 512), dot(lhs, act[:, cols], 0, 0))

    def core_copy(k):
        d = 2 * ((x + k) % NX) + 1 - c
        return send(pbuf.at[d], crecv.at[k], s_c.at[k], r_c.at[k], sib, seq)

    def x_copy(k):
        xx = (x + k) % NX
        return send(pbuf.at[2 * xx + c], xrecv.at[k - 1], s_x.at[k], r_x.at[k], 2 * xx + c, seq)

    def first(i, carry):
        k = (i + 1) % NX
        d = 2 * ((x + k) % NX) + 1 - c

        def put(cols, v):
            pbuf[d, :, cols] = v.astype(BF16)

        part(d, put)
        core_copy(k).start()
        return carry

    lax.fori_loop(0, NX, first, 0)

    def second(k, carry):
        d = 2 * ((x + k) % NX) + c
        core_copy(k).wait_recv()

        def put(cols, v):
            pbuf[d, :, cols] = (v + crecv[k, :, cols].astype(F32)).astype(BF16)

        part(d, put)
        x_copy(k).start()
        return carry

    lax.fori_loop(1, NX, second, 0)
    core_copy(0).wait_recv()

    def put_own(cols, v):
        acc[:, cols] = v + crecv[0, :, cols].astype(F32)

    part(dp, put_own)

    recv_all(c_in, NY * NZ)
    to_rows(xin, tall)
    for b in range(BW):
        for h in range(2):
            v = tall[h, pl.ds(b, NC, stride=BW), :].astype(BF16)
            tall2[h, pl.ds(b, NC, stride=BW), :] = dot(coarse[2 * y + h], v, 0, 0)
    from_rows(tall2, xout)
    c_out = exchange_out(xout, bfine, s_out, r_out, x, c, y, z)
    start_all(c_out, NY * NZ)
    own_out(xout, bfine, x, c, y, z)

    to_rows(moved, tallm)
    for d in range(G):
        v32[d % 2, d // 2, :, GW:] = jnp.zeros((128, GW), F32)
    for h in range(2):
        total = jnp.zeros((NC, NC), F32)
        for b in range(BW):
            at = pl.ds(b, NC, stride=BW)
            total = total + dot(tall[h, at, :].astype(BF16), tallm[h, at, :].astype(BF16), 1, 1)
        v32[h, y, :, GW:] = total

    for k in range(1, NX):
        x_copy(k).wait_recv()

    def add_x(i, carry):
        at = pl.ds(pl.multiple_of(i * 16, 16), 16)
        v = acc[at, :]
        for k in range(NX - 1):
            v = v + xrecv[k, at, :].astype(F32)
        acc[at, :] = v
        return carry

    lax.fori_loop(0, 8, add_x, 0)

    def y_copy(k):
        yy = (y + k) % NY
        return send(ysend.at[yy], yrecv.at[k - 1], s_y.at[k], r_y.at[k], dp, yy * NZ + z)

    for yy in range(NY):
        ysend[yy] = acc[32 * yy : 32 * yy + 32, :].astype(BF16)
    start_all(y_copy, NY)
    recv_all(y_copy, NY)
    for part_row in range(4):
        at = pl.ds(pl.multiple_of(32 * y + 8 * part_row, 8), 8)
        v = acc[at, :]
        for k in range(NY - 1):
            v = v + yrecv[k, 8 * part_row : 8 * part_row + 8, :].astype(F32)
        zbuf[2 * part_row] = v[:4]
        zbuf[2 * part_row + 1] = v[4:]

    def z_copy(k):
        zz = (z + k) % NZ
        return send(zbuf.at[zz], zrecv.at[k - 1], s_z.at[k], r_z.at[k], dp, y * NZ + zz)

    start_all(z_copy, NZ)

    recv_all(c_out, NY * NZ)
    for g in range(G):
        cols = slice(g * GW, (g + 1) * GW)
        total = jnp.zeros((NB, NB), F32)
        for a in range(BL):
            v = bfine[a, :, cols]
            total = total + dot(v, hid[a, :, cols], 1, 1)
            bhid[a, :, cols] = bafter[a, :, cols] * mixed[a, :, cols].astype(F32) + dot(
                fine[g], v, 0, 0
            )
        v32[g % 2, g // 2, :, :GW] = total

    def last(i, total):
        a = i // 8
        at = pl.ds(pl.multiple_of((i % 8) * 16, 16), 16)
        v = tok[a, at, :].astype(F32)
        inv = lax.rsqrt(jnp.mean(v * v, axis=-1, keepdims=True) + EPS)
        normed = v * inv
        bh = bhid[a, at, :]
        w1 = bh * gain[...]
        prod = bh * normed
        center = jnp.mean(prod * gain[...], axis=-1, keepdims=True)
        gin[a, at, :] = (bafter[a, at, :] + inv * (w1 - normed * center)).astype(BF16)
        return total + prod[:8] + prod[8:]

    gm = lax.fori_loop(0, BL * 8, last, jnp.zeros((8, D), F32))
    gm = jnp.sum(gm, axis=0, keepdims=True)

    def c_small():
        return send(v16, vc, ts.at[0, 0], tr.at[0, 0], sib, seq)

    def c_gain():
        return send(gc.at[c], gc.at[c], gs.at[0, 0], gr.at[0, 0], sib, seq)

    for d in range(G):
        gc[pl.ds(c, 1), d : d + 1, :GW] = gm[:, d * GW : (d + 1) * GW].reshape(1, 1, GW)
    gc[pl.ds(c, 1), :, GW:] = glm[...].reshape(1, 8, GW)
    c_gain().start()
    v16[...] = v32[1 - c].astype(BF16)
    c_small().start()

    recv_all(z_copy, NZ)
    scale = 1.0 / math.sqrt(8 * NC * NB)
    v = zbuf[z]
    for k in range(NZ - 1):
        v = v + zrecv[k]
    v = v * scale
    ogu[...] = v[:, : 2 * FF]
    odn[...] = v[:, 2 * FF :]

    def x_small(k):
        xx = (x + k) % NX
        return send(vxs.at[xx], vx.at[k - 1], ts.at[1, k], tr.at[1, k], 2 * xx + c, seq)

    def x_gain(k):
        xx = (x + k) % NX
        return send(gx.at[x], gx.at[x], gs.at[1, k], gr.at[1, k], 2 * xx + c, seq)

    def y_small(k):
        yy = (y + k) % NY
        return send(vys.at[yy], vy.at[k - 1], ts.at[2, k], tr.at[2, k], dp, yy * NZ + z)

    def y_gain(k):
        yy = (y + k) % NY
        return send(gy.at[y], gy.at[y], gs.at[2, k], gr.at[2, k], dp, yy * NZ + z)

    def z_small(k):
        zz = (z + k) % NZ
        return send(vz.at[zz], vzr.at[k - 1], ts.at[3, k], tr.at[3, k], dp, y * NZ + zz)

    def z_gain(k):
        zz = (z + k) % NZ
        return send(gz.at[z], gz.at[z], gs.at[3, k], gr.at[3, k], dp, y * NZ + zz)

    c_gain().wait_recv()
    gx[x] = gc[0] + gc[1]
    start_all(x_gain, NX)
    c_small().wait_recv()
    for xx in range(NX):
        vxs[xx] = (v32[c, xx] + vc[xx].astype(F32)).astype(BF16)
    start_all(x_small, NX)
    v2[...] = v32[c, x] + vc[x].astype(F32)

    recv_all(x_gain, NX)
    gy[y] = (gx[0] + gx[1]) + (gx[2] + gx[3])
    start_all(y_gain, NY)
    recv_all(x_small, NX)
    v = v2[...]
    for k in range(NX - 1):
        v = v + vx[k].astype(F32)
    v2[...] = v
    for yy in range(NY):
        vys[yy] = v[32 * yy : 32 * yy + 32].astype(BF16)
    start_all(y_small, NY)

    recv_all(y_gain, NY)
    gz[z] = (gy[0] + gy[1]) + (gy[2] + gy[3])
    start_all(z_gain, NZ)
    recv_all(y_small, NY)
    v = v2[pl.ds(pl.multiple_of(32 * y, 32), 32), :]
    for k in range(NY - 1):
        v = v + vy[k].astype(F32)
    for zz in range(NZ):
        vz[zz] = v[4 * zz : 4 * zz + 4]
    start_all(z_small, NZ)
    recv_all(z_small, NZ)
    v = vz[z]
    for k in range(NZ - 1):
        v = v + vzr[k]
    az[z] = v

    def z_back(k):
        zz = (z + k) % NZ
        return send(az.at[z], az.at[z], ts.at[4, k], tr.at[4, k], dp, y * NZ + zz)

    def y_back(k):
        yy = (y + k) % NY
        return send(ay.at[y], ay.at[y], ts.at[5, k], tr.at[5, k], dp, yy * NZ + z)

    def x_back(k):
        xx = (x + k) % NX
        return send(every.at[c, x], every.at[c, x], ts.at[6, k], tr.at[6, k], 2 * xx + c, seq)

    def c_back(k):
        xx = (x + NX - k) % NX
        return send(every.at[c, xx], every.at[c, xx], ts.at[7, k], tr.at[7, k], sib, seq)

    start_all(z_back, NZ)
    recv_all(z_gain, NZ)
    v = gz[0]
    for zz in range(1, NZ):
        v = v + gz[zz]
    ogain[...] = v * scale
    recv_all(z_back, NZ)
    for zz in range(NZ):
        v3[4 * zz : 4 * zz + 4, :] = az[zz]
    ay[y] = v3[...].astype(BF16)
    start_all(y_back, NY)
    recv_all(y_back, NY)
    for yy in range(NY):
        every[c, x, 32 * yy : 32 * yy + 32, :] = ay[yy]
    start_all(x_back, NX)
    c_back(0).start()
    for k in range(1, NX):
        x_back(k).wait_recv()
        c_back(k).start()
    for k in range(NX):
        c_back(k).wait_recv()
    lower = lax.broadcasted_iota(jnp.int32, (128, 128), 0) >= lax.broadcasted_iota(
        jnp.int32, (128, 128), 1
    )
    small = 1.0 / math.sqrt(8 * NC * GW)
    for d in range(G):
        v = every[d % 2, d // 2].astype(F32) * small
        ofine[d] = jnp.where(lower, v[:, :GW], 0.0)
        ocoarse[d] = jnp.where(lower, v[:, GW:], 0.0)

    sent_all(c_in, NY * NZ)
    sent_all(c_out, NY * NZ)
    for k in range(NX):
        core_copy(k).wait_send()
        c_back(k).wait_send()
    for copy, n in (
        (x_copy, NX), (y_copy, NY), (z_copy, NZ),
        (x_small, NX), (y_small, NY), (z_small, NZ),
        (x_gain, NX), (y_gain, NY), (z_gain, NZ),
        (z_back, NZ), (y_back, NY), (x_back, NX),
    ):
        sent_all(copy, n)
    c_small().wait_send()
    c_gain().wait_send()


def vmem(n):
    return [pl.BlockSpec(memory_space=pltpu.VMEM)] * n


def dma(*shape):
    return pltpu.SemaphoreType.DMA(shape)


def norm_rows(values):
    scale_inv = lax.rsqrt(jnp.mean(values * values, axis=-1, keepdims=True) + EPS)
    return (values * scale_inv, scale_inv)


def norm_back(upstream, normed, scale_inv):
    return scale_inv * (upstream - normed * jnp.mean(upstream * normed, axis=-1, keepdims=True))


def on_device(tokens, cotangent, gain_mix, gain_mlp, fine, coarse, w_gate_up, w_down):
    tok = tokens.reshape(BL, NB, D)
    gain = gain_mix.reshape(1, D)
    S = jax.ShapeDtypeStruct
    V = pltpu.VMEM
    mixed, hid, moved, fgu, fdn = pl.pallas_call(
        forward_kernel,
        name="mix_forward",
        out_shape=(
            S((BL, NB, D), BF16),
            S((BL, NB, D), BF16),
            S((NC, BW, QW), BF16),
            S((D, 2 * FF), BF16),
            S((D, FF), BF16),
        ),
        in_specs=vmem(6),
        out_specs=tuple(vmem(5)),
        scratch_shapes=[
            V((BL, NB, D), BF16),
            V((NC, BW, QW), BF16),
            V((2, NC * BW, GW), F32),
            V((2, NC * BW, GW), F32),
            V((NZ, 4, WC), BF16),
            V((32, WC), F32),
            dma(32), dma(32), dma(32), dma(32),
            dma(8), dma(8), dma(2, 4), dma(2, 4), dma(2, 4), dma(2, 4), dma(2, 4), dma(2, 4),
        ],
        compiler_params=pltpu.CompilerParams(
            collective_id=0, has_side_effects=True, vmem_limit_bytes=60 * 1024 * 1024
        ),
    )(tok, gain, fine, coarse, w_gate_up, w_down)

    source = tokens[0].astype(F32)
    mixed32 = mixed.reshape(ROWS, D).astype(F32)
    hid32 = hid.reshape(ROWS, D).astype(F32)
    after_mix = source + mixed32 * hid32
    normed_mlp, inv_mlp = norm_rows(after_mix)
    mlp_in = (normed_mlp * gain_mlp).astype(BF16)
    both = jnp.dot(mlp_in, fgu, preferred_element_type=F32)
    gate_pre = both[:, :FF]
    upward = both[:, FF:]
    squash = jax.nn.sigmoid(gate_pre)
    silu_gate = gate_pre * squash
    silu_slope = squash * (1.0 + gate_pre * (1.0 - squash))
    act = (silu_gate * upward).astype(BF16)
    projected = dot(act, fdn, 1, 1)
    layer = (after_mix + projected).astype(BF16)
    cot = cotangent[0]
    back_act = jnp.dot(cot, fdn, preferred_element_type=F32).astype(BF16).astype(F32)
    bboth = jnp.concatenate(
        [back_act * upward * silu_slope, back_act * silu_gate], axis=1
    ).astype(BF16)
    back_mlp_in = dot(bboth, fgu, 1, 1)
    glm = jnp.sum(back_mlp_in * normed_mlp, axis=0)
    bafter = cot.astype(F32) + norm_back(back_mlp_in * gain_mlp, normed_mlp, inv_mlp)
    bm = (bafter * hid32).astype(BF16)

    gin, ogu, odn, ofine, ocoarse, ogain = pl.pallas_call(
        backward_kernel,
        name="mix_backward",
        out_shape=(
            S((BL, NB, D), BF16),
            S((4, 2 * FF), F32),
            S((4, FF), F32),
            S((G, NB, NB), F32),
            S((G, NC, NC), F32),
            S((8, 256), F32),
        ),
        in_specs=vmem(14),
        out_specs=tuple(vmem(6)),
        scratch_shapes=[
            V((NC, BW, QW), BF16),
            V((NC, BW, QW), BF16),
            V((BL, NB, D), BF16),
            V((BL, NB, D), F32),
            V((2, NC * BW, GW), F32),
            V((2, NC * BW, GW), F32),
            V((2, NC * BW, GW), F32),
            V((8, 128, WC), BF16),
            V((4, 128, WC), BF16),
            V((3, 128, WC), BF16),
            V((128, WC), F32),
            V((4, 32, WC), BF16),
            V((3, 32, WC), BF16),
            V((8, 4, WC), F32),
            V((7, 4, WC), F32),
            V((2, 4, 128, 256), F32),
            V((4, 128, 256), BF16),
            V((4, 128, 256), BF16),
            V((4, 128, 256), BF16),
            V((3, 128, 256), BF16),
            V((128, 256), F32),
            V((4, 32, 256), BF16),
            V((3, 32, 256), BF16),
            V((8, 4, 256), F32),
            V((7, 4, 256), F32),
            V((8, 4, 256), F32),
            V((32, 256), F32),
            V((4, 32, 256), BF16),
            V((2, 4, 128, 256), BF16),
            V((2, 8, 256), F32),
            V((4, 8, 256), F32),
            V((4, 8, 256), F32),
            V((8, 8, 256), F32),
            dma(32), dma(32), dma(32), dma(32),
            dma(4), dma(4), dma(4), dma(4), dma(4), dma(4), dma(8), dma(8),
            dma(8, 8), dma(8, 8), dma(4, 8), dma(4, 8),
        ],
        compiler_params=pltpu.CompilerParams(
            collective_id=1, has_side_effects=True, vmem_limit_bytes=60 * 1024 * 1024
        ),
    )(
        bm.reshape(BL, NB, D), moved, fine, coarse, mlp_in, bboth, cot, act,
        bafter.reshape(BL, NB, D), mixed, hid, tok, gain, glm.reshape(8, GW),
    )
    return (
        layer.reshape(1, ROWS, D),
        gin.reshape(1, ROWS, D),
        ogu,
        odn,
        ofine,
        ocoarse,
        ogain[:, :GW].reshape(D),
        ogain[:, GW:].reshape(D),
    )


def solution(mesh):
    rows = P("dp", "seq", None)
    weights = P(("dp", "seq"), None)
    return jax.shard_map(
        on_device,
        mesh=mesh,
        in_specs=(rows, rows, P(), P(), P(), P(), weights, weights),
        out_specs=(rows, rows, weights, weights, P(), P(), P(), P()),
        check_vma=False,
    )
```

time: 649 us -> 219 us (0.34)
  waiting for transfers between devices: 367 us -> 0 us
  Pallas kernels: 0 us -> 195 us
  blocking collectives: 147 us -> 0 us
  local copies, waits for them, and re-layouts: 43.1 us -> 6.96 us
  matrix products: 32.6 us -> 9.91 us
  other arithmetic: 27 us -> 6.45 us
  starting transfers between devices: 16.7 us -> 0 us
  between operations: 14.1 us -> 0.78 us
    pallas_call x0 -> x2, Pallas kernels: none -> 195 us  [the longest x1 122 us: on_device(): pl.pallas_call(backward_kernel, name='mix_backward', out_shape=(S((BL, NB...]
    unnamed x4 -> x0, waiting for transfers between devices: 195 us -> none
    all_gather x2 -> x0, waiting for transfers between devices: 134 us -> none  [the longest x1 111 us: on_device(): lax.all_gather(w_gate_up, ('dp', 'seq'), axis=0, tiled=True)]
    psum x1 -> x0, blocking collectives: 77.5 us -> none  [on_device(): lax.psum((fine_term, coarse_term, gain_mix_term, gain_mlp_term), ('dp', '...]
    all_to_all x2 -> x0, blocking collectives: 69.3 us -> none  [into_coarse(): lax.all_to_all(block_data, 'seq', split_axis=1, concat_axis=0, tiled=True)]
    all_to_all x2 -> x0, waiting for transfers between devices: 37.5 us -> none  [into_fine(): lax.all_to_all(block_data, 'seq', split_axis=0, concat_axis=1, tiled=True)]
    dot_general x12 -> x4, matrix products: 32.6 us -> 9.91 us  [the longest x2 5.53 us: dot(): lax.dot_general(a, b, (((ca,), (cb,)), ((), ())), preferred_element_type=...]
    all_to_all x2 -> x0, starting transfers between devices: 16.6 us -> none  [into_fine(): lax.all_to_all(block_data, 'seq', split_axis=0, concat_axis=1, tiled=True)]
  transfers between devices with their start and end apart: 5 -> 0, of which waited for: 5 -> 0; matrix products, arithmetic and copies ran while one was open for 9% -> 0% of each run, Pallas kernels for 0% -> 0%
where the time goes in v1:
time: 219 us
  Pallas kernels  195 us (89%)
  matrix products  9.91 us (5%)
  local copies, waits for them, and re-layouts  6.96 us (3%)
  other arithmetic  6.45 us (3%)
    pallas_call x1, Pallas kernels, on_device(): pl.pallas_call(backward_kernel, name='mix_backward', out_shape=(S((BL, NB...  122 us
    pallas_call x1, Pallas kernels, on_device(): pl.pallas_call(forward_kernel, name='mix_forward', out_shape=(S((BL, NB,...  73.4 us
    unnamed x29, local copies, waits for them, and re-layouts  5.59 us
    dot_general x2, matrix products, dot(): lax.dot_general(a, b, (((ca,), (cb,)), ((), ())), preferred_element_type=...  5.53 us

profile of v1, /device:TPU:1, one launch (start us, length us, event | category | flops | bytes accessed | tf_op | source)
XLA Modules:
  0.0 219.3 jit_solution(6984747405667530132)
XLA Ops:
  0.6 0.0 copy-start
  0.6 73.4 %mix_forward.1 = (bf16[4,128,1024]{2,1,0:T(8,128)(2,1)}, bf16[4,128,1024]{2,1,0:T(8,128)(2,1)}, bf16[128,16,256]{2,1,0:T(8,128)(2,1)}, bf16[1024,2048]{1,0:T(8,128)(2,1)}, bf16[1024,1024]{1,0:T(8,128)(2,1)}) custom-call(bf16[4,128,1024]{2,1,0:T(8,128)(2,1)} %bitcast.47, f32[1,1024]{1,0:T(1,128)} %bitcast.53, bf16[8,128,128]{2,1,0:T(8,128)(2,1)} %fine.3, ...), custom_call_target="tpu_custom_call" | custom-call | tf_op jit(solution)/shard_map/mix_forward/pallas_call | solution.py:587
  74.1 0.0 copy-done
  74.1 0.0 copy-start.8
  74.1 0.0 copy-start.10
  74.1 2.2 %multiply_reduce_fusion.2 = (f32[512]{0:T(512)S(1)}, f32[512,1024]{1,0:T(8,128)S(1)}) fusion(bf16[4,128,1024]{2,1,0:T(8,128)(2,1)} %get-tuple-element.20.hid, bf16[4,128,1024]{2,1,0:T(8,128)(2,1)} %get-tuple-element.19.mixed, bf16[1,512,1024]{2,1,0:T(8,128)(2,1)S(1)} %copy-done), kind=kLoop, calls=%fused_computation.18 | loop fusion | flops 3669504 | bytes 5244928 | tf_op jit(solution)/shard_map/reduce_sum | solution.py:574
  76.4 0.0 copy-done.8
  76.4 0.2 multiply_convert_fusion.1.mlp_in
  76.6 0.3 copy-done.10
  76.9 0.0 copy-start.2
  77.0 0.0 copy-start.3
  77.0 0.0 copy-start.11
  77.0 2.3 %fusion.10 = f32[512,2048]{1,0:T(8,128)S(1)} fusion(bf16[512,1024]{1,0:T(8,128)(2,1)S(1)} %multiply_convert_fusion.1.mlp_in, bf16[1024,2048]{1,0:T(8,128)(2,1)S(1)} %copy-done.10), kind=kOutput, calls=%fused_computation.27 | convolution fusion | flops 2147483648 | bytes 9437184 | tf_op jit(solution)/shard_map/dot_general | solution.py:620
  79.3 0.0 copy-done.2
  79.3 0.0 copy-done.3
  79.3 0.0 copy-done.11
  79.3 2.0 fusion.3
  81.4 0.0 copy-start.4
  81.4 2.3 %fusion.6 = bf16[1,512,1024]{2,1,0:T(8,128)(2,1)} fusion(f32[512,1024]{1,0:T(8,128)S(1)} %get-tuple-element.35, bf16[512,1024]{1,0:T(8,128)(2,1)S(1)} %get-tuple-element.38.act, bf16[1024,1024]{1,0:T(8,128)(2,1)S(1)} %copy-done.11), kind=kOutput, calls=%fused_computation.20 | convolution fusion | flops 1074790400 | bytes 6291456 | tf_op jit(solution)/shard_map/dot_general | solution.py:63
  83.7 0.0 copy-done.4
  83.7 3.2 %multiply_reduce_fusion = (f32[1024]{0:T(1024)}, f32[512]{0:T(512)S(1)}, f32[512,1024]{1,0:T(8,128)S(1)}) fusion(f32[512,1024]{1,0:T(8,128)S(1)} %get-tuple-element.35, f32[512]{0:T(512)S(1)} %add_rsqrt_fusion, f32[1024]{0:T(1024)S(1)} %copy-done.8, bf16[1024,2048]{1,0:T(8,128)(2,1)S(1)} %copy-done.10, bf16[512,1024]{1,0:T(8,128)(2,1)S(1)} %get-tuple-element.37, ...), kind=kOutput, calls=%fused_computation.10 | convolution fusion | flops 2154822144 | bytes 10498048 | tf_op jit(solution)/shard_map/dot_general | solution.py:63
  86.9 0.0 copy-start.1
  86.9 1.5 pad_maximum_fusion.bboth
  88.4 0.2 copy-done.1
  88.5 2.5 %fusion.1 = (bf16[512,1024]{1,0:T(8,128)(2,1)}, f32[512,1024]{1,0:T(8,128)}) fusion(bf16[4,128,1024]{2,1,0:T(8,128)(2,1)S(1)} %copy-done.1, f32[512]{0:T(512)S(1)} %broadcast_multiply_fusion, f32[512,1024]{1,0:T(8,128)S(1)} %get-tuple-element.35, f32[512,1024]{1,0:T(8,128)S(1)} %get-tuple-element.41, f32[1024]{0:T(1024)S(1)} %copy-done.8, ...), kind=kLoop, calls=%fused_computation.3 | loop fusion | flops 5242880 | bytes 9445376 | tf_op jit(solution)/shard_map/convert_element_type | solution.py:637
  91.0 121.7 %mix_backward.1 = (bf16[4,128,1024]{2,1,0:T(8,128)(2,1)}, f32[4,2048]{1,0:T(4,128)}, f32[4,1024]{1,0:T(4,128)}, f32[8,128,128]{2,1,0:T(8,128)}, f32[8,128,128]{2,1,0:T(8,128)}, /*index=5*/f32[8,256]{1,0:T(8,128)}) custom-call(bf16[4,128,1024]{2,1,0:T(8,128)(2,1)} %bitcast.51, bf16[128,16,256]{2,1,0:T(8,128)(2,1)} %get-tuple-element.23.moved, ...), custom_call_target="tpu_custom_call" | custom-call | tf_op jit(solution)/shard_map/mix_backward/pallas_call | solution.py:639
  212.8 0.0 copy-start.7
  212.8 0.0 copy-start.9
  212.8 0.0 copy-start.6
  212.8 0.0 copy-start.5
  212.8 1.4 slice_bitcast_fusion
  214.2 2.3 %copy.23 = bf16[1,512,1024]{2,1,0:T(8,128)(2,1)} copy(bf16[1,512,1024]{2,1,0:T(8,128)(2,1)} %bitcast.52) | data formatting | bytes 2097152
  216.4 0.0 copy-done.7
  216.5 0.6 copy.24
  217.1 0.0 copy-done.9
  217.1 0.6 copy.25
  217.7 0.0 copy-done.6
  217.7 0.8 copy.26
  218.5 0.0 copy-done.5
  218.5 0.8 copy.27
  (2 shorter events, 0.0 us)
Async XLA Ops:
  0.6 73.5 %copy-start = (bf16[1,512,1024]{2,1,0:T(8,128)(2,1)S(1)}, bf16[1,512,1024]{2,1,0:T(8,128)(2,1)}, u32[]{:S(2)}) copy-start(bf16[1,512,1024]{2,1,0:T(8,128)(2,1)} %param.8) | copy-start | bytes 3145732
  74.1 2.3 %copy-start.8 = (f32[1024]{0:T(1024)S(1)}, f32[1024]{0:T(1024)}, u32[]{:S(2)}) copy-start(f32[1024]{0:T(1024)} %param.11) | copy-start | bytes 12292
  74.1 2.8 %copy-start.10 = (bf16[1024,2048]{1,0:T(8,128)(2,1)S(1)}, bf16[1024,2048]{1,0:T(8,128)(2,1)}, u32[]{:S(2)}) copy-start(bf16[1024,2048]{1,0:T(8,128)(2,1)} %get-tuple-element.21) | copy-start | bytes 12582916
  76.9 2.3 %copy-start.2 = (bf16[512,1024]{1,0:T(8,128)(2,1)}, bf16[512,1024]{1,0:T(8,128)(2,1)S(1)}, u32[]{:S(2)}) copy-start(bf16[512,1024]{1,0:T(8,128)(2,1)S(1)} %multiply_convert_fusion.1.mlp_in) | copy-start | bytes 3145732
  77.0 2.4 %copy-start.3 = (bf16[1,512,1024]{2,1,0:T(8,128)(2,1)S(1)}, bf16[1,512,1024]{2,1,0:T(8,128)(2,1)}, u32[]{:S(2)}) copy-start(bf16[1,512,1024]{2,1,0:T(8,128)(2,1)} %param.9) | copy-start | bytes 3145732
  77.0 2.4 %copy-start.11 = (bf16[1024,1024]{1,0:T(8,128)(2,1)S(1)}, bf16[1024,1024]{1,0:T(8,128)(2,1)}, u32[]{:S(2)}) copy-start(bf16[1024,1024]{1,0:T(8,128)(2,1)} %get-tuple-element.22) | copy-start | bytes 6291460
  81.4 2.3 %copy-start.4 = (bf16[512,1024]{1,0:T(8,128)(2,1)}, bf16[512,1024]{1,0:T(8,128)(2,1)S(1)}, u32[]{:S(2)}) copy-start(bf16[512,1024]{1,0:T(8,128)(2,1)S(1)} %get-tuple-element.38.act) | copy-start | bytes 3145732
  86.9 1.6 copy-start.1
  212.8 3.7 %copy-start.7 = (f32[4,2048]{1,0:T(4,128)S(1)}, f32[4,2048]{1,0:T(4,128)}, u32[]{:S(2)}) copy-start(f32[4,2048]{1,0:T(4,128)} %get-tuple-element.52) | copy-start | bytes 98308
  212.8 4.3 %copy-start.9 = (f32[4,1024]{1,0:T(4,128)S(1)}, f32[4,1024]{1,0:T(4,128)}, u32[]{:S(2)}) copy-start(f32[4,1024]{1,0:T(4,128)} %get-tuple-element.53) | copy-start | bytes 49156
  212.8 4.9 %copy-start.6 = (f32[8,128,128]{2,1,0:T(8,128)S(1)}, f32[8,128,128]{2,1,0:T(8,128)}, u32[]{:S(2)}) copy-start(f32[8,128,128]{2,1,0:T(8,128)} %get-tuple-element.54) | copy-start | bytes 1572868
  212.8 5.7 %copy-start.5 = (f32[8,128,128]{2,1,0:T(8,128)S(1)}, f32[8,128,128]{2,1,0:T(8,128)}, u32[]{:S(2)}) copy-start(f32[8,128,128]{2,1,0:T(8,128)} %get-tuple-element.55) | copy-start | bytes 1572868

commit v2 on v0

v2 whole, which is shorter than its diff:
```python
import math

import jax
import jax.numpy as jnp
from jax import lax
from jax.experimental import pallas as pl
from jax.experimental.pallas import tpu as pltpu
from jax.sharding import PartitionSpec as P

D = 1024
FF = 1024
NB = 128
NC = 128
GW = 128
G = 8
NX, NY, NZ = 4, 4, 8
BL = 4
QW = 256
BW = 16
ROWS = BL * NB
WC = 3 * FF
EPS = 1e-05
MESH = pl.DeviceIdType.MESH
F32 = jnp.float32
BF16 = jnp.bfloat16


def place():
    dp = lax.axis_index("dp")
    seq = lax.axis_index("seq")
    return dp // 2, dp % 2, seq // NZ, seq % NZ


def send(src, dst, ssem, rsem, dp, seq):
    return pltpu.make_async_remote_copy(
        src_ref=src,
        dst_ref=dst,
        send_sem=ssem,
        recv_sem=rsem,
        device_id=(dp, seq),
        device_id_type=MESH,
    )


def greet(x, c, y, z):
    bar = pltpu.get_barrier_semaphore()

    def one(dp, seq):
        pl.semaphore_signal(bar, inc=1, device_id=(dp, seq), device_id_type=MESH)

    def plane(k, carry):
        one(2 * x + c, ((y + k // NZ) % NY) * NZ + (z + k % NZ) % NZ)
        return carry

    lax.fori_loop(1, NY * NZ, plane, 0)
    for k in range(1, 2 * NX):
        one((2 * x + c + k) % (2 * NX), y * NZ + z)
    return bar, NY * NZ - 1 + 2 * NX - 1


def dot(a, b, ca=1, cb=0):
    return lax.dot_general(a, b, (((ca,), (cb,)), ((), ())), preferred_element_type=F32)


def exchange_in(src, dst, ssem, rsem, x, c, y, z):
    me = y * NZ + z

    def part(slot, first, count, lane, width):
        def copy(k):
            ty = (y + k // NZ) % NY
            tz = (z + k % NZ) % NZ
            return send(
                src.at[
                    pl.ds(first, count),
                    pl.ds(pl.multiple_of(BW * tz, BW), BW),
                    pl.ds(pl.multiple_of(QW * ty + lane, GW), width),
                ],
                dst.at[pl.ds(BL * me + first, count), :, pl.ds(lane, width)],
                ssem.at[slot, k],
                rsem.at[slot, k],
                2 * x + c,
                ty * NZ + tz,
            )

        return copy

    return part


def exchange_out(src, dst, ssem, rsem, x, c, y, z):
    def part(slot, first, count, lane, width):
        def copy(k):
            ty = (y + k // NZ) % NY
            tz = (z + k % NZ) % NZ
            to = ty * NZ + tz
            return send(
                src.at[pl.ds(BL * to + first, count), :, pl.ds(lane, width)],
                dst.at[
                    pl.ds(first, count),
                    pl.ds(pl.multiple_of(BW * z, BW), BW),
                    pl.ds(pl.multiple_of(QW * y + lane, GW), width),
                ],
                ssem.at[slot, k],
                rsem.at[slot, k],
                2 * x + c,
                to,
            )

        return copy

    return part


def start_all(copy, n):
    def body(k, carry):
        copy(k).start()
        return carry

    lax.fori_loop(1, n, body, 0)


def recv_all(copy, n):
    def body(k, carry):
        copy(k).wait_recv()
        return carry

    lax.fori_loop(1, n, body, 0)


def sent_all(copy, n):
    def body(k, carry):
        copy(k).wait_send()
        return carry

    lax.fori_loop(1, n, body, 0)


def to_rows(src, tall, h):
    def body(i, carry):
        v = src[pl.ds(8 * i, 8), :, GW * h : GW * h + GW].reshape(8 * BW, GW).astype(F32)
        tall[h, pl.ds(pl.multiple_of(8 * BW * i, 8 * BW), 8 * BW), :] = v
        return carry

    lax.fori_loop(0, NC // 8, body, 0)


def from_rows(tall, dst, h):
    def body(i, carry):
        v = tall[h, pl.ds(pl.multiple_of(8 * BW * i, 8 * BW), 8 * BW), :].astype(BF16)
        dst[pl.ds(8 * i, 8), :, GW * h : GW * h + GW] = v.reshape(8, BW, GW)
        return carry

    lax.fori_loop(0, NC // 8, body, 0)


def columns(tall, h, first, count):
    at = [tall[h, pl.ds(b, NC, stride=BW), :].astype(BF16) for b in range(first, first + count)]
    return jnp.concatenate(at, axis=1)


def coarse_mix(factor, tall, out, h, side):
    for b in range(0, BW, 4):
        v = dot(factor, columns(tall, h, b, 4), side, 0)
        for n in range(4):
            out[h, pl.ds(b + n, NC, stride=BW), :] = v[:, n * GW : n * GW + GW]


def own_in(src, dst, x, c, y, z):
    dst[pl.ds(BL * (y * NZ + z), BL)] = src[
        :, pl.ds(pl.multiple_of(BW * z, BW), BW), pl.ds(pl.multiple_of(QW * y, QW), QW)
    ]


def own_out(src, dst, x, c, y, z):
    dst[:, pl.ds(pl.multiple_of(BW * z, BW), BW), pl.ds(pl.multiple_of(QW * y, QW), QW)] = src[
        pl.ds(BL * (y * NZ + z), BL)
    ]


class SmallSum:
    def __init__(self, refs, sems, gain, x, c, y, z):
        self.v, self.vs, self.vr, self.pieces, self.pr, self.cg, self.full, self.every = refs[:8]
        self.ss, self.rs = sems
        self.gain = gain
        self.dp, self.y, self.z = 2 * x + c, y, z
        self.seq = y * NZ + z

    def plane(self, k):
        return ((self.y + k // NZ) % NY) * NZ + (self.z + k % NZ) % NZ

    def a(self, k):
        to = (self.dp + k) % 8
        return send(self.vs.at[to], self.vr.at[k], self.ss.at[0, k], self.rs.at[0, k], to, self.seq)

    def ga(self, k):
        to = (self.dp + k) % 8
        loc, rec, _, _, gs, gr = self.gain
        return send(loc.at[to], rec.at[k], gs.at[0, k], gr.at[0, k], to, self.seq)

    def b(self, k):
        to = self.plane(k)
        return send(
            self.pieces.at[to], self.pr.at[k], self.ss.at[1, k], self.rs.at[1, k], self.dp, to
        )

    def c(self, k):
        return send(
            self.cg.at[self.seq], self.cg.at[self.seq],
            self.ss.at[2, k], self.rs.at[2, k], self.dp, self.plane(k),
        )

    def d(self, k):
        to = (self.dp + k) % 8
        return send(
            self.every.at[self.dp], self.every.at[self.dp],
            self.ss.at[3, k], self.rs.at[3, k], to, self.seq,
        )

    def gd(self, k):
        to = (self.dp + k) % 8
        _, _, _, ge, gs, gr = self.gain
        return send(ge.at[self.dp], ge.at[self.dp], gs.at[1, k], gr.at[1, k], to, self.seq)

    def start_a(self):
        if self.gain is not None:
            start_all(self.ga, 8)
        for d in range(G):
            self.vs[d] = self.v[d].astype(BF16)
        start_all(self.a, 8)

    def start_b(self):
        if self.gain is not None:
            recv_all(self.ga, 8)
            t = self.gain[0][self.dp]
            for k in range(1, 8):
                t = t + self.gain[1][k]
        recv_all(self.a, 8)
        s = self.v[self.dp]
        for k in range(1, 8):
            s = s + self.vr[k].astype(F32)
        for j in range(NY * NZ):
            self.pieces[j, :4, :] = s[4 * j : 4 * j + 4]
            if self.gain is not None:
                self.pieces[j, 4:, :] = t[:4]
            else:
                self.pieces[j, 4:, :] = jnp.zeros((4, 128), F32)
        start_all(self.b, NY * NZ)

    def start_c(self):
        recv_all(self.b, NY * NZ)
        s = self.pieces[self.seq]
        for k in range(1, NY * NZ):
            s = s + self.pr[k]
        self.cg[self.seq] = s
        start_all(self.c, NY * NZ)

    def start_d(self):
        recv_all(self.c, NY * NZ)
        if self.gain is not None:
            self.gain[3][self.dp] = self.cg[0]
            start_all(self.gd, 8)
        for j in range(NY * NZ):
            self.full[4 * j : 4 * j + 4, :] = self.cg[j, :4, :]
        self.every[self.dp] = self.full[...].astype(BF16)
        start_all(self.d, 8)

    def finish(self):
        recv_all(self.d, 8)
        sent_all(self.a, 8)
        sent_all(self.b, NY * NZ)
        sent_all(self.c, NY * NZ)
        sent_all(self.d, 8)
        if self.gain is not None:
            recv_all(self.gd, 8)
            sent_all(self.ga, 8)
            sent_all(self.gd, 8)


def small_scratch():
    V = pltpu.VMEM
    return [
        V((8, 128, 128), F32),
        V((8, 128, 128), BF16),
        V((8, 128, 128), BF16),
        V((32, 8, 128), F32),
        V((32, 8, 128), F32),
        V((32, 8, 128), F32),
        V((128, 128), F32),
        dma(4, 32),
        dma(4, 32),
    ]


def dma(*shape):
    return pltpu.SemaphoreType.DMA(shape)


def blocks(ref, cols):
    return jnp.concatenate([ref[a, :, cols] for a in range(BL)], axis=1)


def layer_kernel(
    tok, cot, gain, gain2, fine, coarse, wgu, wdn,
    gin, layer, wsum, fevery, cevery, gevery,
    hid, fm, moved, back, mixed, bm, xin, xout, bfine, bhid, tall, tall2, tallm,
    wz, wrow, w,
    after, invs, mlp_in, act, bboth, bmi, glm8,
    pbuf, crecv, xrecv, acc, ysend, yrecv, zbuf, zrecv,
    s_a, r_a, s_b, r_b, s_d, r_d, s_e, r_e,
    s_g, r_g, s_c, r_c, s_x, r_x, s_y, r_y, s_z, r_z,
    gloc, grec, gs, gr,
    *small,
):
    x, c, y, z = place()
    dp = 2 * x + c
    seq = y * NZ + z
    sib = 2 * x + 1 - c
    bar, count = greet(x, c, y, z)
    sf = SmallSum((*small[:7], fevery), small[7:9], (gloc, grec, None, gevery, gs, gr), x, c, y, z)
    sc = SmallSum((*small[9:16], cevery), small[16:18], None, x, c, y, z)

    wz[pl.ds(z, 1), :, : 2 * FF] = wgu[...].reshape(1, 4, 2 * FF)
    wz[pl.ds(z, 1), :, 2 * FF :] = wdn[...].reshape(1, 4, FF)
    HA = slice(0, WC // 2)
    HB = slice(WC // 2, WC)

    def gz(k):
        tz = (z + k) % NZ
        return send(wz.at[z], wz.at[z], s_g.at[0, k], r_g.at[0, k], dp, y * NZ + tz)

    def ga_y(k):
        at = w.at[x, c, y, :, HA]
        return send(at, at, s_g.at[1, k], r_g.at[1, k], dp, ((y + k) % NY) * NZ + z)

    def ga_x(k):
        at = w.at[x, c, :, :, HA]
        return send(at, at, s_g.at[2, k], r_g.at[2, k], 2 * ((x + k) % NX) + c, seq)

    def ga_c(k):
        at = w.at[(x + NX - k) % NX, c, :, :, HA]
        return send(at, at, s_g.at[3, k], r_g.at[3, k], sib, seq)

    def gb_x(k):
        at = w.at[x, c, y, :, HB]
        return send(at, at, s_g.at[4, k], r_g.at[4, k], 2 * ((x + k) % NX) + c, seq)

    def gb_y(k):
        at = w.at[:, c, y, :, HB]
        return send(at, at, s_g.at[5, k], r_g.at[5, k], dp, ((y + k) % NY) * NZ + z)

    def gb_c(k):
        at = w.at[:, c, (y + NY - k) % NY, :, HB]
        return send(at, at, s_g.at[6, k], r_g.at[6, k], sib, seq)

    def norm(i, carry):
        a = i // 4
        at = pl.ds(pl.multiple_of((i % 4) * 32, 32), 32)
        v = tok[a, at, :].astype(F32)
        inv = lax.rsqrt(jnp.mean(v * v, axis=-1, keepdims=True) + EPS)
        hid[a, at, :] = ((v * inv) * gain[...]).astype(BF16)
        return carry

    lax.fori_loop(0, BL * 4, norm, 0)
    pl.semaphore_wait(bar, count)
    start_all(gz, NZ)

    ex_a = exchange_in(fm, moved, s_a, r_a, x, c, y, z)
    for h in range(2):
        for g in range(h, G, 2):
            cols = slice(g * GW, (g + 1) * GW)
            v = dot(fine[g], blocks(hid, cols)).astype(BF16)
            for a in range(BL):
                fm[a, :, cols] = v[:, a * NB : a * NB + NB]
        start_all(ex_a(h, 0, BL, GW * h, GW), NY * NZ)
    own_in(fm, moved, x, c, y, z)

    recv_all(gz, NZ)
    for zz in range(NZ):
        wrow[4 * zz : 4 * zz + 4, :] = wz[zz].astype(F32)
    w[x, c, y] = wrow[...].astype(BF16)
    start_all(ga_y, NY)
    start_all(gb_x, NX)
    recv_all(ga_y, NY)
    start_all(ga_x, NX)
    recv_all(gb_x, NX)
    start_all(gb_y, NY)
    ga_c(0).start()
    gb_c(0).start()

    for h in range(2):
        recv_all(ex_a(h, 0, BL, GW * h, GW), NY * NZ)
        to_rows(moved, tallm, h)
        coarse_mix(coarse[2 * y + h], tallm, tall2, h, 1)
        from_rows(tall2, back, h)
    ex_b = exchange_out(back, mixed, s_b, r_b, x, c, y, z)
    start_all(ex_b(0, 0, 2, 0, QW), NY * NZ)
    start_all(ex_b(1, 2, 2, 0, QW), NY * NZ)
    own_out(back, mixed, x, c, y, z)

    def gather_x(k, carry):
        ga_x(k).wait_recv()
        ga_c(k).start()
        gb_y(k).wait_recv()
        gb_c(k).start()
        return carry

    lax.fori_loop(1, NX, gather_x, 0)
    for k in range(NX):
        ga_c(k).wait_recv()
        gb_c(k).wait_recv()

    glm8[...] = jnp.zeros_like(glm8)
    ex_d = exchange_in(bm, xin, s_d, r_d, x, c, y, z)
    HALF = ROWS // 2

    def mlp(i, carry):
        rows = pl.ds(pl.multiple_of(i * HALF, HALF), HALF)
        recv_all(ex_b(i, 2 * i, 2, 0, QW), NY * NZ)

        def pre(r, carry):
            a = 2 * i + r // 8
            at = pl.ds(pl.multiple_of((r % 8) * 16, 16), 16)
            to = pl.ds(pl.multiple_of(i * HALF + r * 16, 16), 16)
            v = tok[a, at, :].astype(F32) + mixed[a, at, :].astype(F32) * hid[a, at, :].astype(F32)
            inv = lax.rsqrt(jnp.mean(v * v, axis=-1, keepdims=True) + EPS)
            after[to, :] = v
            invs[to, :] = jnp.broadcast_to(inv, (16, 128))
            mlp_in[to, :] = ((v * inv) * gain2[...]).astype(BF16)
            return carry

        lax.fori_loop(0, HALF // 16, pre, 0)

        def hidden(n, carry):
            lane = pl.multiple_of(n * 256, 256)
            cols = pl.ds(lane, 256)
            cols2 = pl.ds(pl.multiple_of(FF + lane, 256), 256)
            cols3 = pl.ds(pl.multiple_of(2 * FF + lane, 256), 256)
            m = mlp_in[rows, :]
            gate = dot(m, w[:, :, :, :, cols].reshape(D, 256))
            up = dot(m, w[:, :, :, :, cols2].reshape(D, 256))
            ba = dot(cot[rows, :], w[:, :, :, :, cols3].reshape(D, 256)).astype(BF16).astype(F32)
            sq = jax.nn.sigmoid(gate)
            sg = gate * sq
            act[rows, cols] = (sg * up).astype(BF16)
            bboth[rows, cols] = (ba * up * (sq * (1.0 + gate * (1.0 - sq)))).astype(BF16)
            bboth[rows, cols2] = (ba * sg).astype(BF16)
            return carry

        lax.fori_loop(0, FF // 256, hidden, 0)

        def up_back(m, carry):
            cols = pl.ds(pl.multiple_of(m * 256, 256), 256)
            bmi[rows, cols] = dot(bboth[rows, :], w[m, :, :, :, : 2 * FF].reshape(256, 2 * FF), 1, 1)
            return carry

        lax.fori_loop(0, D // 256, up_back, 0)

        def post(r, total):
            a = 2 * i + r // 8
            at = pl.ds(pl.multiple_of((r % 8) * 16, 16), 16)
            to = pl.ds(pl.multiple_of(i * HALF + r * 16, 16), 16)
            inv = invs[to, 0:1]
            n2 = after[to, :] * inv
            v = bmi[to, :]
            prod = v * n2
            w2 = v * gain2[...]
            center = jnp.mean(w2 * n2, axis=-1, keepdims=True)
            ba = cot[to, :].astype(F32) + inv * (w2 - n2 * center)
            bmi[to, :] = ba
            bm[a, at, :] = (ba * hid[a, at, :].astype(F32)).astype(BF16)
            return total + prod[:8] + prod[8:]

        glm8[...] = lax.fori_loop(0, HALF // 16, post, glm8[...])

        @pl.when(i == 0)
        def _():
            start_all(ex_d(0, 0, 2, 0, QW), NY * NZ)

        return carry

    lax.fori_loop(0, 2, mlp, 0)
    for h in range(2):
        start_all(ex_d(1 + h, 2, 2, GW * h, GW), NY * NZ)
    own_in(bm, xin, x, c, y, z)

    def part(d, put):
        at = pl.ds(pl.multiple_of(d * 128, 128), 128)
        lhs = mlp_in[:, at]
        for n in range(4):
            cols = slice(512 * n, 512 * n + 512)
            put(cols, dot(lhs, bboth[:, cols], 0, 0))
        lhs = cot[:, at]
        for n in range(2):
            cols = slice(512 * n, 512 * n + 512)
            put(slice(2 * FF + 512 * n, 2 * FF + 512 * n + 512), dot(lhs, act[:, cols], 0, 0))

    def core_copy(k):
        d = 2 * ((x + k) % NX) + 1 - c
        return send(pbuf.at[d], crecv.at[k], s_c.at[k], r_c.at[k], sib, seq)

    def x_copy(k):
        xx = (x + k) % NX
        return send(pbuf.at[2 * xx + c], xrecv.at[k - 1], s_x.at[k], r_x.at[k], 2 * xx + c, seq)

    def first(i, carry):
        k = (i + 1) % NX
        d = 2 * ((x + k) % NX) + 1 - c

        def put(cols, v):
            pbuf[d, :, cols] = v.astype(BF16)

        part(d, put)
        core_copy(k).start()
        return carry

    lax.fori_loop(0, NX, first, 0)

    def second(k, carry):
        d = 2 * ((x + k) % NX) + c
        core_copy(k).wait_recv()

        def put(cols, v):
            pbuf[d, :, cols] = (v + crecv[k, :, cols].astype(F32)).astype(BF16)

        part(d, put)
        x_copy(k).start()
        return carry

    lax.fori_loop(1, NX, second, 0)

    recv_all(ex_d(0, 0, 2, 0, QW), NY * NZ)
    ex_e = exchange_out(xout, bfine, s_e, r_e, x, c, y, z)
    for h in range(2):
        recv_all(ex_d(1 + h, 2, 2, GW * h, GW), NY * NZ)
        to_rows(xin, tall, h)
        coarse_mix(coarse[2 * y + h], tall, tall2, h, 0)
        from_rows(tall2, xout, h)
        start_all(ex_e(h, 0, BL, GW * h, GW), NY * NZ)
    own_out(xout, bfine, x, c, y, z)

    for d in range(G):
        sc.v[d] = jnp.zeros((NC, NC), F32)
    for h in range(2):
        total = jnp.zeros((NC, NC), F32)
        for b in range(0, BW, 4):
            total = total + dot(columns(tall, h, b, 4), columns(tallm, h, b, 4), 1, 1)
        sc.v[2 * y + h] = total
    sc.start_a()

    core_copy(0).wait_recv()

    def put_own(cols, v):
        acc[:, cols] = v + crecv[0, :, cols].astype(F32)

    part(dp, put_own)
    sc.start_b()

    def project(m, carry):
        cols = pl.ds(pl.multiple_of(m * 256, 256), 256)
        v = dot(act[...], w[m, :, :, :, 2 * FF :].reshape(256, FF), 1, 1)
        layer[:, cols] = (after[:, cols] + v).astype(BF16)
        return carry

    lax.fori_loop(0, D // 256, project, 0)
    sc.start_c()

    def y_copy(k):
        yy = (y + k) % NY
        return send(ysend.at[yy], yrecv.at[k - 1], s_y.at[k], r_y.at[k], dp, yy * NZ + z)

    def z_copy(k):
        zz = (z + k) % NZ
        return send(zbuf.at[zz], zrecv.at[k - 1], s_z.at[k], r_z.at[k], dp, y * NZ + zz)

    def weights_y():
        for k in range(1, NX):
            x_copy(k).wait_recv()

        def add_x(i, carry):
            at = pl.ds(pl.multiple_of(i * 16, 16), 16)
            v = acc[at, :]
            for k in range(NX - 1):
                v = v + xrecv[k, at, :].astype(F32)
            acc[at, :] = v
            return carry

        lax.fori_loop(0, 8, add_x, 0)
        for yy in range(NY):
            ysend[yy] = acc[32 * yy : 32 * yy + 32, :].astype(BF16)
        start_all(y_copy, NY)

    def weights_z():
        recv_all(y_copy, NY)
        for q in range(4):
            at = pl.ds(pl.multiple_of(32 * y + 8 * q, 8), 8)
            v = acc[at, :]
            for k in range(NY - 1):
                v = v + yrecv[k, 8 * q : 8 * q + 8, :].astype(F32)
            zbuf[2 * q] = v[:4]
            zbuf[2 * q + 1] = v[4:]
        start_all(z_copy, NZ)

    def last_mix(h):
        recv_all(ex_e(h, 0, BL, GW * h, GW), NY * NZ)
        for g in range(h, G, 2):
            cols = slice(g * GW, (g + 1) * GW)
            v = blocks(bfine, cols)
            sf.v[g] = dot(v, blocks(hid, cols), 1, 1)
            v = dot(fine[g], v, 0, 0)
            for a in range(BL):
                bhid[a, :, cols] = (
                    bmi[a * NB : a * NB + NB, cols] * mixed[a, :, cols].astype(F32)
                    + v[:, a * NB : a * NB + NB]
                )

    last_mix(0)
    last_mix(1)

    def sums(i, total):
        a = i // 8
        at = pl.ds(pl.multiple_of((i % 8) * 16, 16), 16)
        v = tok[a, at, :].astype(F32)
        inv = lax.rsqrt(jnp.mean(v * v, axis=-1, keepdims=True) + EPS)
        prod = bhid[a, at, :] * (v * inv)
        return total + prod[:8] + prod[8:]

    gm = lax.fori_loop(0, BL * 8, sums, jnp.zeros((8, D), F32))
    gm = jnp.sum(gm, axis=0, keepdims=True)
    gl = jnp.sum(glm8[...], axis=0, keepdims=True)
    for d in range(G):
        gloc[d, 0:1, :] = gm[:, d * GW : (d + 1) * GW]
        gloc[d, 1:2, :] = gl[:, d * GW : (d + 1) * GW]
        gloc[d, 2:, :] = jnp.zeros((6, GW), F32)
    sf.start_a()
    weights_y()
    sf.start_b()

    def last(i, carry):
        a = i // 8
        at = pl.ds(pl.multiple_of((i % 8) * 16, 16), 16)
        to = pl.ds(pl.multiple_of(i * 16, 16), 16)
        v = tok[a, at, :].astype(F32)
        inv = lax.rsqrt(jnp.mean(v * v, axis=-1, keepdims=True) + EPS)
        normed = v * inv
        w1 = bhid[a, at, :] * gain[...]
        center = jnp.mean(w1 * normed, axis=-1, keepdims=True)
        gin[a, at, :] = (bmi[to, :] + inv * (w1 - normed * center)).astype(BF16)
        return carry

    lax.fori_loop(0, BL * 8, last, 0)
    sf.start_c()
    weights_z()
    sc.start_d()
    sf.start_d()
    recv_all(z_copy, NZ)
    v = zbuf[z]
    for k in range(NZ - 1):
        v = v + zrecv[k]
    wsum[...] = v

    sent_all(gz, NZ)
    for copy in (ga_y, ga_x, gb_x, gb_y, x_copy, y_copy):
        sent_all(copy, 4)
    for k in range(NX):
        ga_c(k).wait_send()
        gb_c(k).wait_send()
        core_copy(k).wait_send()
    sent_all(z_copy, NZ)
    for h in range(2):
        sent_all(ex_a(h, 0, BL, GW * h, GW), NY * NZ)
        sent_all(ex_b(h, 2 * h, 2, 0, QW), NY * NZ)
        sent_all(ex_d(1 + h, 2, 2, GW * h, GW), NY * NZ)
        sent_all(ex_e(h, 0, BL, GW * h, GW), NY * NZ)
    sent_all(ex_d(0, 0, 2, 0, QW), NY * NZ)
    sc.finish()
    sf.finish()


def finish_kernel(
    gin, layer, wsum, fevery, cevery, gevery,
    ogin, olayer, ogu, odn, ofine, ocoarse, omix, omlp,
):
    olayer[0] = layer[...]
    ogin[0] = gin[...].reshape(ROWS, D)
    scale = 1.0 / math.sqrt(8 * NC * NB)
    ogu[...] = wsum[:, : 2 * FF] * scale
    odn[...] = wsum[:, 2 * FF :] * scale
    lower = lax.broadcasted_iota(jnp.int32, (128, 128), 0) >= lax.broadcasted_iota(
        jnp.int32, (128, 128), 1
    )
    small = 1.0 / math.sqrt(8 * NC * GW)
    for d in range(G):
        ofine[d] = jnp.where(lower, fevery[d].astype(F32) * small, 0.0)
        ocoarse[d] = jnp.where(lower, cevery[d].astype(F32) * small, 0.0)
        omix[:, d * GW : (d + 1) * GW] = gevery[d, 4:5, :] * scale
        omlp[:, d * GW : (d + 1) * GW] = gevery[d, 5:6, :] * scale


def vmem(n):
    return [pl.BlockSpec(memory_space=pltpu.VMEM)] * n


def on_device(tokens, cotangent, gain_mix, gain_mlp, fine, coarse, w_gate_up, w_down):
    S = jax.ShapeDtypeStruct
    V = pltpu.VMEM
    parts = pl.pallas_call(
        layer_kernel,
        name="layer",
        out_shape=(
            S((BL, NB, D), BF16),
            S((ROWS, D), BF16),
            S((4, WC), F32),
            S((G, 128, 128), BF16),
            S((G, 128, 128), BF16),
            S((G, 8, 128), F32),
        ),
        in_specs=vmem(8),
        out_specs=tuple(vmem(6)),
        scratch_shapes=[
            V((BL, NB, D), BF16),
            V((BL, NB, D), BF16),
            V((NC, BW, QW), BF16),
            V((NC, BW, QW), BF16),
            V((BL, NB, D), BF16),
            V((BL, NB, D), BF16),
            V((NC, BW, QW), BF16),
            V((NC, BW, QW), BF16),
            V((BL, NB, D), BF16),
            V((BL, NB, D), F32),
            V((2, NC * BW, GW), F32),
            V((2, NC * BW, GW), F32),
            V((2, NC * BW, GW), F32),
            V((NZ, 4, WC), BF16),
            V((32, WC), F32),
            V((NX, 2, NY, 32, WC), BF16),
            V((ROWS, D), F32),
            V((ROWS, 128), F32),
            V((ROWS, D), BF16),
            V((ROWS, FF), BF16),
            V((ROWS, 2 * FF), BF16),
            V((ROWS, D), F32),
            V((8, D), F32),
            V((8, 128, WC), BF16),
            V((4, 128, WC), BF16),
            V((3, 128, WC), BF16),
            V((128, WC), F32),
            V((4, 32, WC), BF16),
            V((3, 32, WC), BF16),
            V((8, 4, WC), F32),
            V((7, 4, WC), F32),
            dma(2, 32), dma(2, 32), dma(2, 32), dma(2, 32),
            dma(3, 32), dma(3, 32), dma(2, 32), dma(2, 32),
            dma(7, 8), dma(7, 8),
            dma(4), dma(4), dma(4), dma(4), dma(4), dma(4), dma(8), dma(8),
            V((8, 8, 128), F32), V((8, 8, 128), F32), dma(2, 8), dma(2, 8),
            *small_scratch(), *small_scratch(),
        ],
        compiler_params=pltpu.CompilerParams(
            collective_id=0, has_side_effects=True, vmem_limit_bytes=63 * 1024 * 1024
        ),
    )(
        tokens.reshape(BL, NB, D), cotangent.reshape(ROWS, D),
        gain_mix.reshape(1, D), gain_mlp.reshape(1, D), fine, coarse, w_gate_up, w_down,
    )
    gin, layer, ogu, odn, ofine, ocoarse, omix, omlp = pl.pallas_call(
        finish_kernel,
        name="finish",
        out_shape=(
            S((1, ROWS, D), BF16),
            S((1, ROWS, D), BF16),
            S((4, 2 * FF), F32),
            S((4, FF), F32),
            S((G, NB, NB), F32),
            S((G, NC, NC), F32),
            S((1, D), F32),
            S((1, D), F32),
        ),
        in_specs=vmem(6),
        out_specs=tuple(vmem(8)),
    )(*parts)
    return (layer, gin, ogu, odn, ofine, ocoarse, omix.reshape(D), omlp.reshape(D))


def solution(mesh):
    rows = P("dp", "seq", None)
    weights = P(("dp", "seq"), None)
    return jax.shard_map(
        on_device,
        mesh=mesh,
        in_specs=(rows, rows, P(), P(), P(), P(), weights, weights),
        out_specs=(rows, rows, weights, weights, P(), P(), P(), P()),
        check_vma=False,
    )
```

time: 649 us -> 193 us (0.30)
  waiting for transfers between devices: 367 us -> 0 us
  Pallas kernels: 0 us -> 190 us
  blocking collectives: 147 us -> 0 us
  local copies, waits for them, and re-layouts: 43.1 us -> 0 us
  matrix products: 32.6 us -> 0 us
  other arithmetic: 27 us -> 0 us
  starting transfers between devices: 16.7 us -> 0 us
  between operations: 14.1 us -> 0.64 us
    unnamed x4 -> x0, waiting for transfers between devices: 195 us -> none
    pallas_call x0 -> x2, Pallas kernels: none -> 190 us  [the longest x1 187 us: on_device(): pl.pallas_call(layer_kernel, name='layer', out_shape=(S((BL, NB, D), BF16...]
    all_gather x2 -> x0, waiting for transfers between devices: 134 us -> none  [the longest x1 111 us: on_device(): lax.all_gather(w_gate_up, ('dp', 'seq'), axis=0, tiled=True)]
    psum x1 -> x0, blocking collectives: 77.5 us -> none  [on_device(): lax.psum((fine_term, coarse_term, gain_mix_term, gain_mlp_term), ('dp', '...]
    all_to_all x2 -> x0, blocking collectives: 69.3 us -> none  [into_coarse(): lax.all_to_all(block_data, 'seq', split_axis=1, concat_axis=0, tiled=True)]
    all_to_all x2 -> x0, waiting for transfers between devices: 37.5 us -> none  [into_fine(): lax.all_to_all(block_data, 'seq', split_axis=0, concat_axis=1, tiled=True)]
    dot_general x12 -> x0, matrix products: 32.6 us -> none  [the longest x1 5.29 us: on_device(): both = jnp.dot(mlp_in, full_gate_up, preferred_element_type=jnp.float32)]
    all_to_all x2 -> x0, starting transfers between devices: 16.6 us -> none  [into_fine(): lax.all_to_all(block_data, 'seq', split_axis=0, concat_axis=1, tiled=True)]
  transfers between devices with their start and end apart: 5 -> 0, of which waited for: 5 -> 0; matrix products, arithmetic and copies ran while one was open for 9% -> 0% of each run, Pallas kernels for 0% -> 0%
where the time goes in v2:
time: 193 us; the launch traced here: 191 us
  Pallas kernels  190 us (98%)
    pallas_call x1, Pallas kernels, on_device(): pl.pallas_call(layer_kernel, name='layer', out_shape=(S((BL, NB, D), BF16...  187 us

profile of v2, /device:TPU:1, one launch (start us, length us, event | category | flops | bytes accessed | tf_op | source)
XLA Modules:
  0.0 191.0 jit_solution(12221397888196058887)
XLA Ops:
  0.6 187.0 %layer.1 = (bf16[4,128,1024]{2,1,0:T(8,128)(2,1)}, bf16[512,1024]{1,0:T(8,128)(2,1)}, f32[4,3072]{1,0:T(4,128)}, bf16[8,128,128]{2,1,0:T(8,128)(2,1)}, bf16[8,12...) custom-call(bf16[4,128,1024]{2,1,0:T(8,128)(2,1)} %bitcast.6, bf16[512,1024]{1,0:T(8,128)(2,1)} %bitcast.7, f32[1,1024]{1,0:T(1,128)} %bitcast.8, ...), custom_call_target="tpu_custom_call" | custom-call | tf_op jit(solution)/shard_map/layer/pallas_call | solution.py:706
  187.6 3.4 %finish.1 = (bf16[1,512,1024]{2,1,0:T(8,128)(2,1)}, bf16[1,512,1024]{2,1,0:T(8,128)(2,1)}, f32[4,2048]{1,0:T(4,128)}, f32[4,1024]{1,0:T(4,128)}, f32[8,128,128]{...) custom-call(bf16[4,128,1024]{2,1,0:T(8,128)(2,1)} %get-tuple-element.22.gin, ...), custom_call_target="tpu_custom_call" | custom-call | tf_op jit(solution)/shard_map/finish/pallas_call | solution.py:765

commit v3 on v2

--- a/solution.py
+++ b/solution.py
@@ -28,7 +28,11 @@
 def place():
     dp = lax.axis_index("dp")
     seq = lax.axis_index("seq")
-    return dp // 2, dp % 2, seq // NZ, seq % NZ
+    return lax.div(dp, 2), lax.rem(dp, 2), lax.div(seq, NZ), lax.rem(seq, NZ)
+
+
+def shifted(y, z, k):
+    return lax.rem(y + lax.div(k, NZ), NY), lax.rem(z + lax.rem(k, NZ), NZ)
 
 
 def send(src, dst, ssem, rsem, dp, seq):
@@ -49,7 +53,8 @@
         pl.semaphore_signal(bar, inc=1, device_id=(dp, seq), device_id_type=MESH)
 
     def plane(k, carry):
-        one(2 * x + c, ((y + k // NZ) % NY) * NZ + (z + k % NZ) % NZ)
+        ty, tz = shifted(y, z, k)
+        one(2 * x + c, ty * NZ + tz)
         return carry
 
     lax.fori_loop(1, NY * NZ, plane, 0)
@@ -67,8 +72,7 @@
 
     def part(slot, first, count, lane, width):
         def copy(k):
-            ty = (y + k // NZ) % NY
-            tz = (z + k % NZ) % NZ
+            ty, tz = shifted(y, z, k)
             return send(
                 src.at[
                     pl.ds(first, count),
@@ -76,12 +80,15 @@
                     pl.ds(pl.multiple_of(QW * ty + lane, GW), width),
                 ],
                 dst.at[pl.ds(BL * me + first, count), :, pl.ds(lane, width)],
-                ssem.at[slot, k],
-                rsem.at[slot, k],
+                ssem.at[slot],
+                rsem.at[slot],
                 2 * x + c,
                 ty * NZ + tz,
             )
 
+        seen = dst.at[pl.ds(0, count * (NY * NZ - 1)), :, pl.ds(lane, width)]
+        copy.recv = lambda: bulk(seen, rsem.at[slot])
+        copy.sent = lambda: bulk(seen, ssem.at[slot])
         return copy
 
     return part
@@ -90,8 +97,7 @@
 def exchange_out(src, dst, ssem, rsem, x, c, y, z):
     def part(slot, first, count, lane, width):
         def copy(k):
-            ty = (y + k // NZ) % NY
-            tz = (z + k % NZ) % NZ
+            ty, tz = shifted(y, z, k)
             to = ty * NZ + tz
             return send(
                 src.at[pl.ds(BL * to + first, count), :, pl.ds(lane, width)],
@@ -100,15 +106,22 @@
                     pl.ds(pl.multiple_of(BW * z, BW), BW),
                     pl.ds(pl.multiple_of(QW * y + lane, GW), width),
                 ],
-                ssem.at[slot, k],
-                rsem.at[slot, k],
+                ssem.at[slot],
+                rsem.at[slot],
                 2 * x + c,
                 to,
             )
 
+        seen = src.at[pl.ds(0, count * (NY * NZ - 1)), :, pl.ds(lane, width)]
+        copy.recv = lambda: bulk(seen, rsem.at[slot])
+        copy.sent = lambda: bulk(seen, ssem.at[slot])
         return copy
 
     return part
+
+
+def bulk(ref, sem):
+    pltpu.make_async_copy(ref, ref, sem).wait()
 
 
 def start_all(copy, n):
@@ -186,68 +199,71 @@
         self.seq = y * NZ + z
 
     def plane(self, k):
-        return ((self.y + k // NZ) % NY) * NZ + (self.z + k % NZ) % NZ
+        ty, tz = shifted(self.y, self.z, k)
+        return ty * NZ + tz
 
     def a(self, k):
-        to = (self.dp + k) % 8
-        return send(self.vs.at[to], self.vr.at[k], self.ss.at[0, k], self.rs.at[0, k], to, self.seq)
+        to = lax.rem(self.dp + k, 8)
+        return send(self.vs.at[to], self.vr.at[k], self.ss.at[0], self.rs.at[0], to, self.seq)
 
     def ga(self, k):
-        to = (self.dp + k) % 8
+        to = lax.rem(self.dp + k, 8)
         loc, rec, _, _, gs, gr = self.gain
-        return send(loc.at[to], rec.at[k], gs.at[0, k], gr.at[0, k], to, self.seq)
+        return send(loc.at[to], rec.at[k], gs.at[0], gr.at[0], to, self.seq)
 
     def b(self, k):
         to = self.plane(k)
         return send(
-            self.pieces.at[to], self.pr.at[k], self.ss.at[1, k], self.rs.at[1, k], self.dp, to
+            self.pieces.at[to], self.pr.at[k], self.ss.at[1], self.rs.at[1], self.dp, to
         )
 
     def c(self, k):
         return send(
             self.cg.at[self.seq], self.cg.at[self.seq],
-            self.ss.at[2, k], self.rs.at[2, k], self.dp, self.plane(k),
+            self.ss.at[2], self.rs.at[2], self.dp, self.plane(k),
         )
 
     def d(self, k):
-        to = (self.dp + k) % 8
+        to = lax.rem(self.dp + k, 8)
         return send(
             self.every.at[self.dp], self.every.at[self.dp],
-            self.ss.at[3, k], self.rs.at[3, k], to, self.seq,
+            self.ss.at[3], self.rs.at[3], to, self.seq,
         )
 
     def gd(self, k):
-        to = (self.dp + k) % 8
+        to = lax.rem(self.dp + k, 8)
         _, _, _, ge, gs, gr = self.gain
-        return send(ge.at[self.dp], ge.at[self.dp], gs.at[1, k], gr.at[1, k], to, self.seq)
+        return send(ge.at[self.dp], ge.at[self.dp], gs.at[1], gr.at[1], to, self.seq)
 
     def start_a(self):
-        if self.gain is not None:
-            start_all(self.ga, 8)
         for d in range(G):
             self.vs[d] = self.v[d].astype(BF16)
         start_all(self.a, 8)
 
+    def start_gain(self):
+        start_all(self.ga, 8)
+
     def start_b(self):
-        if self.gain is not None:
-            recv_all(self.ga, 8)
-            t = self.gain[0][self.dp]
-            for k in range(1, 8):
-                t = t + self.gain[1][k]
-        recv_all(self.a, 8)
+        bulk(self.vr.at[pl.ds(1, 7)], self.rs.at[0])
         s = self.v[self.dp]
         for k in range(1, 8):
             s = s + self.vr[k].astype(F32)
+        if self.gain is not None:
+            loc, rec, _, _, gs, gr = self.gain
+            bulk(rec.at[pl.ds(1, 7)], gr.at[0])
+            t = loc[self.dp]
+            for k in range(1, 8):
+                t = t + rec[k]
+            t = t[:4]
+        else:
+            t = jnp.zeros((4, 128), F32)
         for j in range(NY * NZ):
             self.pieces[j, :4, :] = s[4 * j : 4 * j + 4]
-            if self.gain is not None:
-                self.pieces[j, 4:, :] = t[:4]
-            else:
-                self.pieces[j, 4:, :] = jnp.zeros((4, 128), F32)
+            self.pieces[j, 4:, :] = t
         start_all(self.b, NY * NZ)
 
     def start_c(self):
-        recv_all(self.b, NY * NZ)
+        bulk(self.pr.at[pl.ds(1, NY * NZ - 1)], self.rs.at[1])
         s = self.pieces[self.seq]
         for k in range(1, NY * NZ):
             s = s + self.pr[k]
@@ -255,7 +271,7 @@
         start_all(self.c, NY * NZ)
 
     def start_d(self):
-        recv_all(self.c, NY * NZ)
+        bulk(self.cg.at[pl.ds(0, NY * NZ - 1)], self.rs.at[2])
         if self.gain is not None:
             self.gain[3][self.dp] = self.cg[0]
             start_all(self.gd, 8)
@@ -265,15 +281,16 @@
         start_all(self.d, 8)
 
     def finish(self):
-        recv_all(self.d, 8)
-        sent_all(self.a, 8)
-        sent_all(self.b, NY * NZ)
-        sent_all(self.c, NY * NZ)
-        sent_all(self.d, 8)
+        bulk(self.every.at[pl.ds(0, 7)], self.rs.at[3])
+        bulk(self.vs.at[pl.ds(0, 7)], self.ss.at[0])
+        bulk(self.pieces.at[pl.ds(0, NY * NZ - 1)], self.ss.at[1])
+        bulk(self.cg.at[pl.ds(0, NY * NZ - 1)], self.ss.at[2])
+        bulk(self.every.at[pl.ds(0, 7)], self.ss.at[3])
         if self.gain is not None:
-            recv_all(self.gd, 8)
-            sent_all(self.ga, 8)
-            sent_all(self.gd, 8)
+            loc, _, _, ge, gs, gr = self.gain
+            bulk(ge.at[pl.ds(0, 7)], gr.at[1])
+            bulk(loc.at[pl.ds(0, 7)], gs.at[0])
+            bulk(ge.at[pl.ds(0, 7)], gs.at[1])
 
 
 def small_scratch():
@@ -286,8 +303,8 @@
         V((32, 8, 128), F32),
         V((32, 8, 128), F32),
         V((128, 128), F32),
-        dma(4, 32),
-        dma(4, 32),
+        dma(4),
+        dma(4),
     ]
 
 
@@ -305,7 +322,7 @@
     hid, fm, moved, back, mixed, bm, xin, xout, bfine, bhid, tall, tall2, tallm,
     wz, wrow, w,
     after, invs, mlp_in, act, bboth, bmi, glm8,
-    pbuf, crecv, xrecv, acc, ysend, yrecv, zbuf, zrecv,
+    pbuf, crecv, xrecv, brecv, acc, accb, ysend, bsend, yrecv, bxrecv, zbuf, zrecv,
     s_a, r_a, s_b, r_b, s_d, r_d, s_e, r_e,
     s_g, r_g, s_c, r_c, s_x, r_x, s_y, r_y, s_z, r_z,
     gloc, grec, gs, gr,
@@ -361,8 +378,6 @@
         return carry
 
     lax.fori_loop(0, BL * 4, norm, 0)
-    pl.semaphore_wait(bar, count)
-    start_all(gz, NZ)
 
     ex_a = exchange_in(fm, moved, s_a, r_a, x, c, y, z)
     for h in range(2):
@@ -371,15 +386,19 @@
             v = dot(fine[g], blocks(hid, cols)).astype(BF16)
             for a in range(BL):
                 fm[a, :, cols] = v[:, a * NB : a * NB + NB]
+        if h == 0:
+            pl.semaphore_wait(bar, count)
+            start_all(gz, NZ)
+        else:
+            recv_all(gz, NZ)
+            for zz in range(NZ):
+                wrow[4 * zz : 4 * zz + 4, :] = wz[zz].astype(F32)
+            w[x, c, y] = wrow[...].astype(BF16)
+            start_all(ga_y, NY)
+            start_all(gb_x, NX)
         start_all(ex_a(h, 0, BL, GW * h, GW), NY * NZ)
     own_in(fm, moved, x, c, y, z)
 
-    recv_all(gz, NZ)
-    for zz in range(NZ):
-        wrow[4 * zz : 4 * zz + 4, :] = wz[zz].astype(F32)
-    w[x, c, y] = wrow[...].astype(BF16)
-    start_all(ga_y, NY)
-    start_all(gb_x, NX)
     recv_all(ga_y, NY)
     start_all(ga_x, NX)
     recv_all(gb_x, NX)
@@ -388,7 +407,7 @@
     gb_c(0).start()
 
     for h in range(2):
-        recv_all(ex_a(h, 0, BL, GW * h, GW), NY * NZ)
+        ex_a(h, 0, BL, GW * h, GW).recv()
         to_rows(moved, tallm, h)
         coarse_mix(coarse[2 * y + h], tallm, tall2, h, 1)
         from_rows(tall2, back, h)
@@ -415,7 +434,7 @@
 
     def mlp(i, carry):
         rows = pl.ds(pl.multiple_of(i * HALF, HALF), HALF)
-        recv_all(ex_b(i, 2 * i, 2, 0, QW), NY * NZ)
+        ex_b(i, 2 * i, 2, 0, QW).recv()
 
         def pre(r, carry):
             a = 2 * i + r // 8
@@ -495,43 +514,115 @@
             put(slice(2 * FF + 512 * n, 2 * FF + 512 * n + 512), dot(lhs, act[:, cols], 0, 0))
 
     def core_copy(k):
-        d = 2 * ((x + k) % NX) + 1 - c
-        return send(pbuf.at[d], crecv.at[k], s_c.at[k], r_c.at[k], sib, seq)
-
-    def x_copy(k):
-        xx = (x + k) % NX
-        return send(pbuf.at[2 * xx + c], xrecv.at[k - 1], s_x.at[k], r_x.at[k], 2 * xx + c, seq)
+        xx = lax.rem(x + k, NX)
+        return send(pbuf.at[xx, 1 - c], crecv.at[k], s_c.at[k], r_c.at[k], sib, seq)
+
+    def xa_copy(k):
+        xx = lax.rem(x + k, NX)
+        return send(
+            pbuf.at[xx, c, :, :, HA], xrecv.at[k - 1], s_x.at[0, k], r_x.at[0, k], 2 * xx + c, seq
+        )
+
+    def yb_copy(k):
+        yy = lax.rem(y + k, NY)
+        return send(
+            pbuf.at[:, c, yy, :, HB], brecv.at[k - 1], s_y.at[0, k], r_y.at[0, k], dp, yy * NZ + z
+        )
+
+    def ya_copy(k):
+        yy = lax.rem(y + k, NY)
+        return send(
+            ysend.at[yy], yrecv.at[k - 1], s_y.at[1, k], r_y.at[1, k], dp, yy * NZ + z
+        )
+
+    def xb_copy(k):
+        xx = lax.rem(x + k, NX)
+        return send(
+            bsend.at[xx], bxrecv.at[k - 1], s_x.at[1, k], r_x.at[1, k], 2 * xx + c, seq
+        )
+
+    def z_copy(k):
+        zz = lax.rem(z + k, NZ)
+        return send(zbuf.at[zz], zrecv.at[k - 1], s_z.at[k], r_z.at[k], dp, y * NZ + zz)
 
     def first(i, carry):
-        k = (i + 1) % NX
-        d = 2 * ((x + k) % NX) + 1 - c
+        xx = lax.rem(x + i + 1, NX)
 
         def put(cols, v):
-            pbuf[d, :, cols] = v.astype(BF16)
-
-        part(d, put)
-        core_copy(k).start()
+            n = cols.stop - cols.start
+            pbuf[xx, 1 - c, :, :, cols] = v.astype(BF16).reshape(NY, 32, n)
+
+        part(2 * xx + 1 - c, put)
+        core_copy(lax.rem(i + 1, NX)).start()
         return carry
 
     lax.fori_loop(0, NX, first, 0)
 
-    def second(k, carry):
-        d = 2 * ((x + k) % NX) + c
+    def second(i, carry):
+        k = lax.rem(i + 1, NX)
+        xx = lax.rem(x + k, NX)
         core_copy(k).wait_recv()
 
         def put(cols, v):
-            pbuf[d, :, cols] = (v + crecv[k, :, cols].astype(F32)).astype(BF16)
-
-        part(d, put)
-        x_copy(k).start()
-        return carry
-
-    lax.fori_loop(1, NX, second, 0)
-
-    recv_all(ex_d(0, 0, 2, 0, QW), NY * NZ)
+            n = cols.stop - cols.start
+            v = v.reshape(NY, 32, n) + crecv[k, :, :, cols].astype(F32)
+            pbuf[xx, c, :, :, cols] = v.astype(BF16)
+
+        part(2 * xx + c, put)
+
+        @pl.when(k != 0)
+        def _():
+            xa_copy(k).start()
+
+        return carry
+
+    lax.fori_loop(0, NX, second, 0)
+    start_all(yb_copy, NY)
+
+    def weights_second():
+        recv_all(xa_copy, NX)
+        recv_all(yb_copy, NY)
+
+        def add(yy, carry):
+            for q in range(2):
+                at = slice(16 * q, 16 * q + 16)
+                v = pbuf[x, c, yy, at, HA].astype(F32)
+                for k in range(NX - 1):
+                    v = v + xrecv[k, yy, at, :].astype(F32)
+                acc[yy, at, :] = v
+                ysend[yy, at, :] = v.astype(BF16)
+                v = pbuf[yy, c, y, at, HB].astype(F32)
+                for k in range(NY - 1):
+                    v = v + brecv[k, yy, at, :].astype(F32)
+                accb[yy, at, :] = v
+                bsend[yy, at, :] = v.astype(BF16)
+            return carry
+
+        lax.fori_loop(0, NX, add, 0)
+        start_all(ya_copy, NY)
+        start_all(xb_copy, NX)
+
+    def weights_third():
+        recv_all(ya_copy, NY)
+        recv_all(xb_copy, NX)
+        for q in range(4):
+            at = slice(8 * q, 8 * q + 8)
+            va = acc[y, at, :]
+            for k in range(NY - 1):
+                va = va + yrecv[k, at, :].astype(F32)
+            vb = accb[x, at, :]
+            for k in range(NX - 1):
+                vb = vb + bxrecv[k, at, :].astype(F32)
+            zbuf[2 * q, :, HA] = va[:4].astype(BF16)
+            zbuf[2 * q + 1, :, HA] = va[4:].astype(BF16)
+            zbuf[2 * q, :, HB] = vb[:4].astype(BF16)
+            zbuf[2 * q + 1, :, HB] = vb[4:].astype(BF16)
+        start_all(z_copy, NZ)
+
+    ex_d(0, 0, 2, 0, QW).recv()
     ex_e = exchange_out(xout, bfine, s_e, r_e, x, c, y, z)
     for h in range(2):
-        recv_all(ex_d(1 + h, 2, 2, GW * h, GW), NY * NZ)
+        ex_d(1 + h, 2, 2, GW * h, GW).recv()
         to_rows(xin, tall, h)
         coarse_mix(coarse[2 * y + h], tall, tall2, h, 0)
         from_rows(tall2, xout, h)
@@ -547,12 +638,6 @@
         sc.v[2 * y + h] = total
     sc.start_a()
 
-    core_copy(0).wait_recv()
-
-    def put_own(cols, v):
-        acc[:, cols] = v + crecv[0, :, cols].astype(F32)
-
-    part(dp, put_own)
     sc.start_b()
 
     def project(m, carry):
@@ -564,57 +649,30 @@
     lax.fori_loop(0, D // 256, project, 0)
     sc.start_c()
 
-    def y_copy(k):
-        yy = (y + k) % NY
-        return send(ysend.at[yy], yrecv.at[k - 1], s_y.at[k], r_y.at[k], dp, yy * NZ + z)
-
-    def z_copy(k):
-        zz = (z + k) % NZ
-        return send(zbuf.at[zz], zrecv.at[k - 1], s_z.at[k], r_z.at[k], dp, y * NZ + zz)
-
-    def weights_y():
-        for k in range(1, NX):
-            x_copy(k).wait_recv()
-
-        def add_x(i, carry):
-            at = pl.ds(pl.multiple_of(i * 16, 16), 16)
-            v = acc[at, :]
-            for k in range(NX - 1):
-                v = v + xrecv[k, at, :].astype(F32)
-            acc[at, :] = v
-            return carry
-
-        lax.fori_loop(0, 8, add_x, 0)
-        for yy in range(NY):
-            ysend[yy] = acc[32 * yy : 32 * yy + 32, :].astype(BF16)
-        start_all(y_copy, NY)
-
-    def weights_z():
-        recv_all(y_copy, NY)
-        for q in range(4):
-            at = pl.ds(pl.multiple_of(32 * y + 8 * q, 8), 8)
-            v = acc[at, :]
-            for k in range(NY - 1):
-                v = v + yrecv[k, 8 * q : 8 * q + 8, :].astype(F32)
-            zbuf[2 * q] = v[:4]
-            zbuf[2 * q + 1] = v[4:]
-        start_all(z_copy, NZ)
-
-    def last_mix(h):
-        recv_all(ex_e(h, 0, BL, GW * h, GW), NY * NZ)
+    weights_second()
+
+    def fine_terms(h):
         for g in range(h, G, 2):
             cols = slice(g * GW, (g + 1) * GW)
-            v = blocks(bfine, cols)
-            sf.v[g] = dot(v, blocks(hid, cols), 1, 1)
-            v = dot(fine[g], v, 0, 0)
+            sf.v[g] = dot(blocks(bfine, cols), blocks(hid, cols), 1, 1)
+
+    def back_hidden(h):
+        for g in range(h, G, 2):
+            cols = slice(g * GW, (g + 1) * GW)
+            v = dot(fine[g], blocks(bfine, cols), 0, 0)
             for a in range(BL):
                 bhid[a, :, cols] = (
                     bmi[a * NB : a * NB + NB, cols] * mixed[a, :, cols].astype(F32)
                     + v[:, a * NB : a * NB + NB]
                 )
 
-    last_mix(0)
-    last_mix(1)
+    ex_e(0, 0, BL, 0, GW).recv()
+    fine_terms(0)
+    back_hidden(0)
+    ex_e(1, 0, BL, GW, GW).recv()
+    fine_terms(1)
+    sf.start_a()
+    back_hidden(1)
 
     def sums(i, total):
         a = i // 8
@@ -631,9 +689,9 @@
         gloc[d, 0:1, :] = gm[:, d * GW : (d + 1) * GW]
         gloc[d, 1:2, :] = gl[:, d * GW : (d + 1) * GW]
         gloc[d, 2:, :] = jnp.zeros((6, GW), F32)
-    sf.start_a()
-    weights_y()
+    sf.start_gain()
     sf.start_b()
+    weights_third()
 
     def last(i, carry):
         a = i // 8
@@ -649,17 +707,16 @@
 
     lax.fori_loop(0, BL * 8, last, 0)
     sf.start_c()
-    weights_z()
     sc.start_d()
     sf.start_d()
     recv_all(z_copy, NZ)
-    v = zbuf[z]
+    v = zbuf[z].astype(F32)
     for k in range(NZ - 1):
-        v = v + zrecv[k]
+        v = v + zrecv[k].astype(F32)
     wsum[...] = v
 
     sent_all(gz, NZ)
-    for copy in (ga_y, ga_x, gb_x, gb_y, x_copy, y_copy):
+    for copy in (ga_y, ga_x, gb_x, gb_y, xa_copy, yb_copy, ya_copy, xb_copy):
         sent_all(copy, 4)
     for k in range(NX):
         ga_c(k).wait_send()
@@ -667,11 +724,11 @@
         core_copy(k).wait_send()
     sent_all(z_copy, NZ)
     for h in range(2):
-        sent_all(ex_a(h, 0, BL, GW * h, GW), NY * NZ)
-        sent_all(ex_b(h, 2 * h, 2, 0, QW), NY * NZ)
-        sent_all(ex_d(1 + h, 2, 2, GW * h, GW), NY * NZ)
-        sent_all(ex_e(h, 0, BL, GW * h, GW), NY * NZ)
-    sent_all(ex_d(0, 0, 2, 0, QW), NY * NZ)
+        ex_a(h, 0, BL, GW * h, GW).sent()
+        ex_b(h, 2 * h, 2, 0, QW).sent()
+        ex_d(1 + h, 2, 2, GW * h, GW).sent()
+        ex_e(h, 0, BL, GW * h, GW).sent()
+    ex_d(0, 0, 2, 0, QW).sent()
     sc.finish()
     sf.finish()
 
@@ -740,19 +797,23 @@
             V((ROWS, 2 * FF), BF16),
             V((ROWS, D), F32),
             V((8, D), F32),
-            V((8, 128, WC), BF16),
-            V((4, 128, WC), BF16),
-            V((3, 128, WC), BF16),
-            V((128, WC), F32),
-            V((4, 32, WC), BF16),
-            V((3, 32, WC), BF16),
-            V((8, 4, WC), F32),
-            V((7, 4, WC), F32),
-            dma(2, 32), dma(2, 32), dma(2, 32), dma(2, 32),
-            dma(3, 32), dma(3, 32), dma(2, 32), dma(2, 32),
+            V((NX, 2, NY, 32, WC), BF16),
+            V((NX, NY, 32, WC), BF16),
+            V((3, NY, 32, WC // 2), BF16),
+            V((3, NX, 32, WC // 2), BF16),
+            V((NY, 32, WC // 2), F32),
+            V((NX, 32, WC // 2), F32),
+            V((NY, 32, WC // 2), BF16),
+            V((NX, 32, WC // 2), BF16),
+            V((3, 32, WC // 2), BF16),
+            V((3, 32, WC // 2), BF16),
+            V((8, 4, WC), BF16),
+            V((7, 4, WC), BF16),
+            dma(2), dma(2), dma(2), dma(2),
+            dma(3), dma(3), dma(2), dma(2),
             dma(7, 8), dma(7, 8),
-            dma(4), dma(4), dma(4), dma(4), dma(4), dma(4), dma(8), dma(8),
-            V((8, 8, 128), F32), V((8, 8, 128), F32), dma(2, 8), dma(2, 8),
+            dma(4), dma(4), dma(2, 4), dma(2, 4), dma(2, 4), dma(2, 4), dma(8), dma(8),
+            V((8, 8, 128), F32), V((8, 8, 128), F32), dma(2), dma(2),
             *small_scratch(), *small_scratch(),
         ],
         compiler_params=pltpu.CompilerParams(

time: 193 us -> 168 us (0.87); the launches traced: 191 us -> 168 us
  Pallas kernels: 190 us -> 168 us
    pallas_call x1, Pallas kernels: 187 us -> 164 us  [on_device(): pl.pallas_call(layer_kernel, name='layer', out_shape=(S((BL, NB, D), BF16...]
where the time goes in v3:
time: 168 us
  Pallas kernels  168 us (100%)
    pallas_call x1, Pallas kernels, on_device(): pl.pallas_call(layer_kernel, name='layer', out_shape=(S((BL, NB, D), BF16...  164 us
    pallas_call x1, Pallas kernels, on_device(): pl.pallas_call(finish_kernel, name='finish', out_shape=(S((1, ROWS, D), B...  3.43 us

profile of v3, /device:TPU:1, one launch (start us, length us, event | category | flops | bytes accessed | tf_op | source)
XLA Modules:
  0.0 168.2 jit_solution(17469902491979328475)
XLA Ops:
  0.6 164.1 %layer.1 = (bf16[4,128,1024]{2,1,0:T(8,128)(2,1)}, bf16[512,1024]{1,0:T(8,128)(2,1)}, f32[4,3072]{1,0:T(4,128)}, bf16[8,128,128]{2,1,0:T(8,128)(2,1)}, bf16[8,12...) custom-call(bf16[4,128,1024]{2,1,0:T(8,128)(2,1)} %bitcast.6, bf16[512,1024]{1,0:T(8,128)(2,1)} %bitcast.7, f32[1,1024]{1,0:T(1,128)} %bitcast.8, ...), custom_call_target="tpu_custom_call" | custom-call | tf_op jit(solution)/shard_map/layer/pallas_call | solution.py:763
  164.8 3.4 %finish.1 = (bf16[1,512,1024]{2,1,0:T(8,128)(2,1)}, bf16[1,512,1024]{2,1,0:T(8,128)(2,1)}, f32[4,2048]{1,0:T(4,128)}, f32[4,1024]{1,0:T(4,128)}, f32[8,128,128]{...) custom-call(bf16[4,128,1024]{2,1,0:T(8,128)(2,1)} %get-tuple-element.22.gin, ...), custom_call_target="tpu_custom_call" | custom-call | tf_op jit(solution)/shard_map/finish/pallas_call | solution.py:826

commit v4 on v3

--- a/solution.py
+++ b/solution.py
@@ -324,7 +324,7 @@
     after, invs, mlp_in, act, bboth, bmi, glm8,
     pbuf, crecv, xrecv, brecv, acc, accb, ysend, bsend, yrecv, bxrecv, zbuf, zrecv,
     s_a, r_a, s_b, r_b, s_d, r_d, s_e, r_e,
-    s_g, r_g, s_c, r_c, s_x, r_x, s_y, r_y, s_z, r_z,
+    s_g, r_g, s_x0, r_x0, s_y0, r_y0, s_c, r_c, s_x, r_x, s_y, r_y, s_z, r_z,
     gloc, grec, gs, gr,
     *small,
 ):
@@ -349,9 +349,9 @@
         at = w.at[x, c, y, :, HA]
         return send(at, at, s_g.at[1, k], r_g.at[1, k], dp, ((y + k) % NY) * NZ + z)
 
-    def ga_x(k):
-        at = w.at[x, c, :, :, HA]
-        return send(at, at, s_g.at[2, k], r_g.at[2, k], 2 * ((x + k) % NX) + c, seq)
+    def ga_x(k, j=0):
+        at = w.at[x, c, lax.rem(y + NY - j, NY), :, HA]
+        return send(at, at, s_x0.at[j, k], r_x0.at[j, k], 2 * lax.rem(x + k, NX) + c, seq)
 
     def ga_c(k):
         at = w.at[(x + NX - k) % NX, c, :, :, HA]
@@ -361,9 +361,9 @@
         at = w.at[x, c, y, :, HB]
         return send(at, at, s_g.at[4, k], r_g.at[4, k], 2 * ((x + k) % NX) + c, seq)
 
-    def gb_y(k):
-        at = w.at[:, c, y, :, HB]
-        return send(at, at, s_g.at[5, k], r_g.at[5, k], dp, ((y + k) % NY) * NZ + z)
+    def gb_y(k, j=0):
+        at = w.at[lax.rem(x + NX - j, NX), c, y, :, HB]
+        return send(at, at, s_y0.at[j, k], r_y0.at[j, k], dp, lax.rem(y + k, NY) * NZ + z)
 
     def gb_c(k):
         at = w.at[:, c, (y + NY - k) % NY, :, HB]
@@ -396,13 +396,18 @@
             w[x, c, y] = wrow[...].astype(BF16)
             start_all(ga_y, NY)
             start_all(gb_x, NX)
+            start_all(ga_x, NX)
+            start_all(gb_y, NY)
         start_all(ex_a(h, 0, BL, GW * h, GW), NY * NZ)
     own_in(fm, moved, x, c, y, z)
 
-    recv_all(ga_y, NY)
-    start_all(ga_x, NX)
-    recv_all(gb_x, NX)
-    start_all(gb_y, NY)
+    for j in (1, 3, 2):
+        ga_y(j).wait_recv()
+        for k in (1, 3, 2):
+            ga_x(k, j).start()
+        gb_x(j).wait_recv()
+        for k in (1, 3, 2):
+            gb_y(k, j).start()
     ga_c(0).start()
     gb_c(0).start()
 
@@ -416,14 +421,13 @@
     start_all(ex_b(1, 2, 2, 0, QW), NY * NZ)
     own_out(back, mixed, x, c, y, z)
 
-    def gather_x(k, carry):
-        ga_x(k).wait_recv()
+    for k in (1, 3, 2):
+        for j in range(NY):
+            ga_x(k, j).wait_recv()
         ga_c(k).start()
-        gb_y(k).wait_recv()
+        for j in range(NX):
+            gb_y(k, j).wait_recv()
         gb_c(k).start()
-        return carry
-
-    lax.fori_loop(1, NX, gather_x, 0)
     for k in range(NX):
         ga_c(k).wait_recv()
         gb_c(k).wait_recv()
@@ -716,7 +720,11 @@
     wsum[...] = v
 
     sent_all(gz, NZ)
-    for copy in (ga_y, ga_x, gb_x, gb_y, xa_copy, yb_copy, ya_copy, xb_copy):
+    for k in range(1, NX):
+        for j in range(NY):
+            ga_x(k, j).wait_send()
+            gb_y(k, j).wait_send()
+    for copy in (ga_y, gb_x, xa_copy, yb_copy, ya_copy, xb_copy):
         sent_all(copy, 4)
     for k in range(NX):
         ga_c(k).wait_send()
@@ -738,19 +746,26 @@
     ogin, olayer, ogu, odn, ofine, ocoarse, omix, omlp,
 ):
     olayer[0] = layer[...]
-    ogin[0] = gin[...].reshape(ROWS, D)
-    scale = 1.0 / math.sqrt(8 * NC * NB)
-    ogu[...] = wsum[:, : 2 * FF] * scale
-    odn[...] = wsum[:, 2 * FF :] * scale
-    lower = lax.broadcasted_iota(jnp.int32, (128, 128), 0) >= lax.broadcasted_iota(
-        jnp.int32, (128, 128), 1
-    )
-    small = 1.0 / math.sqrt(8 * NC * GW)
-    for d in range(G):
-        ofine[d] = jnp.where(lower, fevery[d].astype(F32) * small, 0.0)
-        ocoarse[d] = jnp.where(lower, cevery[d].astype(F32) * small, 0.0)
-        omix[:, d * GW : (d + 1) * GW] = gevery[d, 4:5, :] * scale
-        omlp[:, d * GW : (d + 1) * GW] = gevery[d, 5:6, :] * scale
+    ogin[0] = gin[0]
+
+    @pl.when(pl.program_id(0) == 0)
+    def _():
+        scale = 1.0 / math.sqrt(8 * NC * NB)
+        ogu[...] = wsum[:, : 2 * FF] * scale
+        odn[...] = wsum[:, 2 * FF :] * scale
+        lower = lax.broadcasted_iota(jnp.int32, (128, 128), 0) >= lax.broadcasted_iota(
+            jnp.int32, (128, 128), 1
+        )
+        small = 1.0 / math.sqrt(8 * NC * GW)
+        for d in range(G):
+            ofine[d] = jnp.where(lower, fevery[d].astype(F32) * small, 0.0)
+            ocoarse[d] = jnp.where(lower, cevery[d].astype(F32) * small, 0.0)
+            omix[:, d * GW : (d + 1) * GW] = gevery[d, 4:5, :] * scale
+            omlp[:, d * GW : (d + 1) * GW] = gevery[d, 5:6, :] * scale
+
+
+def whole(*shape):
+    return pl.BlockSpec(shape, lambda i: (0,) * len(shape))
 
 
 def vmem(n):
@@ -811,7 +826,7 @@
             V((7, 4, WC), BF16),
             dma(2), dma(2), dma(2), dma(2),
             dma(3), dma(3), dma(2), dma(2),
-            dma(7, 8), dma(7, 8),
+            dma(7, 8), dma(7, 8), dma(4, 4), dma(4, 4), dma(4, 4), dma(4, 4),
             dma(4), dma(4), dma(2, 4), dma(2, 4), dma(2, 4), dma(2, 4), dma(8), dma(8),
             V((8, 8, 128), F32), V((8, 8, 128), F32), dma(2), dma(2),
             *small_scratch(), *small_scratch(),
@@ -836,8 +851,18 @@
             S((1, D), F32),
             S((1, D), F32),
         ),
-        in_specs=vmem(6),
-        out_specs=tuple(vmem(8)),
+        grid=(BL,),
+        in_specs=[
+            pl.BlockSpec((1, NB, D), lambda i: (i, 0, 0)),
+            pl.BlockSpec((NB, D), lambda i: (i, 0)),
+            whole(4, WC), whole(G, 128, 128), whole(G, 128, 128), whole(G, 8, 128),
+        ],
+        out_specs=(
+            pl.BlockSpec((1, NB, D), lambda i: (0, i, 0)),
+            pl.BlockSpec((1, NB, D), lambda i: (0, i, 0)),
+            whole(4, 2 * FF), whole(4, FF), whole(G, NB, NB), whole(G, NC, NC),
+            whole(1, D), whole(1, D),
+        ),
     )(*parts)
     return (layer, gin, ogu, odn, ofine, ocoarse, omix.reshape(D), omlp.reshape(D))
 

time: 168 us -> 162 us (0.964)
  Pallas kernels: 168 us -> 161 us
    pallas_call x1, Pallas kernels: 164 us -> 157 us  [on_device(): pl.pallas_call(layer_kernel, name='layer', out_shape=(S((BL, NB, D), BF16...]
where the time goes in v4:
time: 162 us
  Pallas kernels  161 us (99%)
    pallas_call x1, Pallas kernels, on_device(): pl.pallas_call(layer_kernel, name='layer', out_shape=(S((BL, NB, D), BF16...  157 us
    pallas_call x1, Pallas kernels, on_device(): pl.pallas_call(finish_kernel, name='finish', out_shape=(S((1, ROWS, D), B...  4.45 us

profile of v4, /device:TPU:1, one launch (start us, length us, event | category | flops | bytes accessed | tf_op | source)
XLA Modules:
  0.0 162.0 jit_solution(7471217728188308729)
XLA Ops:
  0.6 156.9 %layer.1 = (bf16[4,128,1024]{2,1,0:T(8,128)(2,1)}, bf16[512,1024]{1,0:T(8,128)(2,1)}, f32[4,3072]{1,0:T(4,128)}, bf16[8,128,128]{2,1,0:T(8,128)(2,1)}, bf16[8,12...) custom-call(bf16[4,128,1024]{2,1,0:T(8,128)(2,1)} %bitcast.6, bf16[512,1024]{1,0:T(8,128)(2,1)} %bitcast.7, f32[1,1024]{1,0:T(1,128)} %bitcast.8, ...), custom_call_target="tpu_custom_call" | custom-call | tf_op jit(solution)/shard_map/layer/pallas_call | solution.py:778
  157.5 4.4 %finish.1 = (bf16[1,512,1024]{2,1,0:T(8,128)(2,1)}, bf16[1,512,1024]{2,1,0:T(8,128)(2,1)}, f32[4,2048]{1,0:T(4,128)}, f32[4,1024]{1,0:T(4,128)}, f32[8,128,128]{...) custom-call(bf16[4,128,1024]{2,1,0:T(8,128)(2,1)} %get-tuple-element.22.gin, ...), custom_call_target="tpu_custom_call" | custom-call | tf_op jit(solution)/shard_map/finish/pallas_call | solution.py:841
